TPU v7x, 32 devices: a whole 2x2x4 slice. The times are simulated.
32 devices in a mesh: rep: 8 (over y, x, core), fsdp: 4 (over z).
Axes of the slice: x: 2, y: 2, z: 4, core: 2. Of those that a mesh axis runs over, the one named last changes fastest.
Arguments:
- tokens: bfloat16 [8, 1024, 1024], P('rep', 'fsdp'), may hold values from -12 to 12
- cotangent: bfloat16 [8, 1024, 1024], P('rep', 'fsdp'), may hold values from -6 to 6
- qkv_weight: bfloat16 [1024, 3072], P('fsdp'), may hold values from -4 to 4
- out_weight: bfloat16 [1024, 1024], P('fsdp'), may hold values from -0.375 to 0.375
- up_weight: bfloat16 [1024, 4096], P('fsdp'), may hold values from -0.1875 to 0.1875
- down_weight: bfloat16 [1024, 4096], P('fsdp'), may hold values from -0.09375 to 0.09375
- ln_gain: bfloat16 [1024], P('fsdp'), may hold values from 0.5 to 1.5
- ln_bias: bfloat16 [1024], P('fsdp'), may hold values from -1.25 to 1.25
- up_bias: bfloat16 [4096], P('fsdp'), may hold values from -3 to 3
- down_bias: bfloat16 [1024], P('fsdp'), may hold values from -1.75 to 1.75
- qkv_moment: float32 [1024, 3072], P('fsdp'), may hold values from -24 to 24
- out_moment: float32 [1024, 1024], P('fsdp'), may hold values from -24 to 24
- up_moment: float32 [1024, 4096], P('fsdp'), may hold values from -24 to 24
- down_moment: float32 [1024, 4096], P('fsdp'), may hold values from -24 to 24
- gain_moment: float32 [1024], P('fsdp'), may hold values from -24 to 24
- beta_moment: float32 [1024], P('fsdp'), may hold values from -24 to 24
- up_bias_moment: float32 [4096], P('fsdp'), may hold values from -24 to 24
- down_bias_moment: float32 [1024], P('fsdp'), may hold values from -24 to 24
Outputs:
- block_out: bfloat16 [8, 1024, 1024], P('rep', 'fsdp')
- input_grad: float32 [8, 1024, 1024], P('rep', 'fsdp')
- qkv_grad: float32 [1024, 3072], P('fsdp')
- out_grad: float32 [1024, 1024], P('fsdp')
- up_grad: float32 [1024, 4096], P('fsdp')
- down_grad: float32 [1024, 4096], P('fsdp')
- gain_grad: float32 [1024], P('fsdp')
- beta_grad: float32 [1024], P('fsdp')
- up_bias_grad: float32 [4096], P('fsdp')
- down_bias_grad: float32 [1024], P('fsdp')
- qkv_new: float32 [1024, 3072], P('fsdp')
- out_new: float32 [1024, 1024], P('fsdp')
- up_new: float32 [1024, 4096], P('fsdp')
- down_new: float32 [1024, 4096], P('fsdp')
- gain_new: float32 [1024], P('fsdp')
- beta_new: float32 [1024], P('fsdp')
- up_bias_new: float32 [4096], P('fsdp')
- down_bias_new: float32 [1024], P('fsdp')
- qkv_moment_new: float32 [1024, 3072], P('fsdp')
- out_moment_new: float32 [1024, 1024], P('fsdp')
- up_moment_new: float32 [1024, 4096], P('fsdp')
- down_moment_new: float32 [1024, 4096], P('fsdp')
- gain_moment_new: float32 [1024], P('fsdp')
- beta_moment_new: float32 [1024], P('fsdp')
- up_bias_moment_new: float32 [4096], P('fsdp')
- down_bias_moment_new: float32 [1024], P('fsdp')
All inputs are finite; a program needn't handle non-finite values.
Results may differ from a plain program's by a relative error of at most 0.011.
Values may be sent and summed in bfloat16 or wider, within the bound.
No kernel may reach another device: no remote copies, remote signals or barrier semaphores. Data moves between devices by JAX's collectives and lax.ppermute only.
A program may use at most 320 MiB of HBM per device.

v0:
```python
import math

import jax
import jax.numpy as jnp
from jax import lax
from jax.experimental import pallas as pl
from jax.experimental.pallas import tpu as pltpu
from jax.sharding import PartitionSpec as P


HEAD_DIM = 64
ROT = 32
NS = 5
QB = 256

MOMENTUM_RATE = 0.9
MATRIX_RATE = 0.05
VECTOR_RATE = 0.002
COEF_A = 3.4445
COEF_B = -4.775
COEF_C = 2.0315

BF = jnp.bfloat16
F32 = jnp.float32


def contract(left, right, left_dim, right_dim):
    return lax.dot_general(
        left, right, (((left_dim,), (right_dim,)), ((), ())), preferred_element_type=F32
    )


def after(x, *others):
    return lax.optimization_barrier((x,) + others)[0]


def z_neighbours(x, nf):
    right = lax.ppermute(x, "fsdp", [(i, i + 1) for i in range(nf - 1)])
    left = lax.ppermute(x, "fsdp", [(i, i - 1) for i in range(1, nf)])
    return right, left


def z_gather(x, near, nf):
    f = lax.axis_index("fsdp")
    length = x.shape[0]
    right, left = near
    from_left, from_right = [right], [left]
    for step in range(1, nf - 1):
        from_left.append(lax.ppermute(right, "fsdp", [(i, i + step) for i in range(1, nf - step)]))
        from_right.append(lax.ppermute(left, "fsdp", [(i, i - step) for i in range(step, nf - 1)]))
    line = jnp.concatenate(from_left[::-1] + [x] + from_right, axis=0)
    return lax.dynamic_slice_in_dim(line, (nf - 1 - f) * length, nf * length, 0)


def z_exchange(x):
    return lax.all_to_all(x, "fsdp", split_axis=0, concat_axis=0, tiled=True)


def xor_swap(x, mask, nr):
    return lax.ppermute(x, "rep", [(i, i ^ mask) for i in range(nr)])


def rep_bit(bit):
    return (lax.axis_index("rep") >> bit) & 1


def high_bits(nr):
    return list(range(1, nr.bit_length() - 1))


def place(index, nr):
    return (index & 1) * (nr // 2) + (index >> 1)


def plane_pieces(x, axis, nr):
    order = high_bits(nr)
    middle = x.shape[axis] // 2

    def halves(part):
        return lax.slice_in_dim(part, 0, middle, axis=axis), lax.slice_in_dim(part, middle, 2 * middle, axis=axis)

    if len(order) == 2:
        one, two = 1 << order[0], 1 << order[1]
        near, far = xor_swap(x, one, nr), xor_swap(x, two, nr)
        both = (xor_swap(halves(far)[0], one, nr), xor_swap(halves(near)[1], two, nr))
        return {0: (x,), one: (near,), two: (far,), one | two: both}
    sides = []
    for part, bits in zip(halves(x), (order[::-1], order)):
        held = {0: part}
        for bit in bits:
            for distance in list(held):
                held[distance | (1 << bit)] = xor_swap(held[distance], 1 << bit, nr)
        sides.append(held)
    return {distance: (sides[0][distance], sides[1][distance]) for distance in sides[0]}


def with_partner(pieces, nr):
    found = dict(pieces)
    for distance, parts in pieces.items():
        found[distance | 1] = tuple(xor_swap(part, 1, nr) for part in parts)
    return found


def listed(pieces):
    return [(d, n, len(pieces[d]), part) for d in sorted(pieces) for n, part in enumerate(pieces[d])]


def halve(x, axis, bit, nr):
    mine = lax.dynamic_index_in_dim(x, rep_bit(bit), axis, keepdims=False)
    other = lax.dynamic_index_in_dim(x, 1 - rep_bit(bit), axis, keepdims=False)
    return mine + xor_swap(other.astype(BF), 1 << bit, nr).astype(F32)


def plane_sum(x, order, nr):
    held = high_bits(nr)
    x = x.reshape((2,) * len(held) + x.shape[1:])
    for bit in order:
        x = halve(x, sum(1 for b in held if b > bit), bit, nr)
        held.remove(bit)
    return x


def plane_sum_small(x, nr):
    for bit in range(nr.bit_length() - 1):
        x = x + xor_swap(x, 1 << bit, nr)
    return x


def rotary_tables(length):
    lane = jnp.arange(2 * HEAD_DIM, dtype=jnp.int32) % HEAD_DIM
    half = ROT // 2
    inverse = 10000.0 ** (-(2.0 * (lane % half).astype(F32)) / ROT)
    angles = jnp.arange(length, dtype=jnp.int32).astype(F32)[:, None] * inverse[None, :]
    cosine = jnp.where(lane < ROT, jnp.cos(angles), 1.0)
    sine = jnp.sin(angles)
    from_low = jnp.where((lane >= half) & (lane < ROT), sine, 0.0)
    from_high = jnp.where(lane < half, -sine, 0.0)
    return cosine, from_low, from_high


def turn(x, cosine, from_low, from_high):
    half = ROT // 2
    width = x.shape[1]
    return x * cosine + pltpu.roll(x, half, 1) * from_low + pltpu.roll(x, width - half, 1) * from_high


def attend_kernel(qf_ref, kf_ref, vf_ref, c_ref, lo_ref, hi_ref, q_ref, k_ref, v_ref, p_ref, o_ref):
    length = qf_ref.shape[0]
    cosine, low, high = c_ref[...], lo_ref[...], hi_ref[...]
    q_ref[...] = (turn(qf_ref[...], cosine, low, high).astype(BF).astype(F32) * HEAD_DIM ** (-0.5)).astype(BF)
    k_ref[...] = turn(kf_ref[...], cosine, low, high).astype(BF)
    v_ref[...] = vf_ref[...].astype(BF)
    row = lax.broadcasted_iota(jnp.int32, (QB, QB), 0)
    col = lax.broadcasted_iota(jnp.int32, (QB, QB), 1)
    for h in range(2):
        lanes = slice(h * HEAD_DIM, (h + 1) * HEAD_DIM)
        for i in range(length // QB):
            rows = slice(i * QB, (i + 1) * QB)
            seen = (i + 1) * QB
            s = contract(q_ref[rows, lanes], k_ref[:seen, lanes], 1, 1)
            last = jnp.where(row >= col, s[:, i * QB :], -1e30)
            s = last if i == 0 else jnp.concatenate([s[:, : i * QB], last], axis=1)
            e = jnp.exp(s - jnp.max(s, axis=1, keepdims=True))
            p = (e / jnp.sum(e, axis=1, keepdims=True)).astype(BF)
            p_ref[h, rows, :seen] = p
            o_ref[rows, lanes] = contract(p, v_ref[:seen, lanes], 1, 0).astype(BF)


def attend(projected, tables, width):
    length = projected.shape[0]
    pairs = width // (2 * HEAD_DIM)
    block = (length, 2 * HEAD_DIM)

    def at(third):
        return pl.BlockSpec(block, lambda h: (0, third * pairs + h))

    whole = pl.BlockSpec(block, lambda h: (0, 0))
    mine = pl.BlockSpec(block, lambda h: (0, h))
    piece = jax.ShapeDtypeStruct((length, width), BF)
    return pl.pallas_call(
        attend_kernel,
        grid=(pairs,),
        in_specs=[at(0), at(1), at(2), whole, whole, whole],
        out_specs=[mine, mine, mine, pl.BlockSpec((2, length, length), lambda h: (h, 0, 0)), mine],
        out_shape=[piece, piece, piece, jax.ShapeDtypeStruct((2 * pairs, length, length), BF), piece],
        name="attend",
    )(projected, projected, projected, *tables)


def attend_back_kernel(q_ref, k_ref, v_ref, p_ref, do_ref, c_ref, lo_ref, hi_ref, dq_ref, dk_ref, dv_ref, ds_ref, acc_ref):
    length = q_ref.shape[0]
    blocks = length // QB
    for h in range(2):
        lanes = slice(h * HEAD_DIM, (h + 1) * HEAD_DIM)
        for i in range(blocks):
            rows = slice(i * QB, (i + 1) * QB)
            seen = (i + 1) * QB
            p = p_ref[h, rows, :seen].astype(F32)
            row = lax.broadcasted_iota(jnp.int32, (QB, seen), 0) + i * QB
            col = lax.broadcasted_iota(jnp.int32, (QB, seen), 1)
            p = jnp.where(row >= col, p, 0.0)
            dp = contract(do_ref[rows, lanes], v_ref[:seen, lanes], 1, 1)
            ds = (p * (dp - jnp.sum(p * dp, axis=1, keepdims=True))).astype(BF)
            ds_ref[rows, :seen] = ds
            acc_ref[0, rows, lanes] = contract(ds, k_ref[:seen, lanes], 1, 0) * HEAD_DIM ** (-0.5)
        for j in range(blocks):
            cols = slice(j * QB, (j + 1) * QB)
            rest = slice(j * QB, length)
            acc_ref[1, cols, lanes] = contract(ds_ref[rest, cols], q_ref[rest, lanes], 0, 0)
            acc_ref[2, cols, lanes] = contract(p_ref[h, rest, cols], do_ref[rest, lanes], 0, 0)
    cosine, low, high = c_ref[...], -lo_ref[...], -hi_ref[...]
    dq_ref[...] = turn(acc_ref[0], cosine, low, high).astype(BF)
    dk_ref[...] = turn(acc_ref[1], cosine, low, high).astype(BF)
    dv_ref[...] = acc_ref[2].astype(BF)


def attend_back(q, k, v, probs, d_mixed, tables):
    length, width = q.shape
    pairs = width // (2 * HEAD_DIM)
    block = (length, 2 * HEAD_DIM)
    whole = pl.BlockSpec(block, lambda h: (0, 0))
    mine = pl.BlockSpec(block, lambda h: (0, h))
    piece = jax.ShapeDtypeStruct((length, width), BF)
    return pl.pallas_call(
        attend_back_kernel,
        grid=(pairs,),
        in_specs=[mine, mine, mine, pl.BlockSpec((2, length, length), lambda h: (h, 0, 0)), mine, whole, whole, whole],
        out_specs=[mine, mine, mine],
        out_shape=[piece, piece, piece],
        scratch_shapes=[pltpu.VMEM((length, length), BF), pltpu.VMEM((3,) + block, F32)],
        name="attend_back",
    )(q, k, v, probs, d_mixed, *tables)


def split(x):
    high = x.astype(BF)
    return high, (x - high.astype(F32)).astype(BF)


def upper(count):
    return [(i, j) for i in range(count) for j in range(i, count)]


def gram_of(pieces):
    entries = listed(pieces)
    slots = sorted(pieces)
    size = sum(part.shape[0] for part in pieces[0])
    wide = pieces[0][0].shape[1]
    count = size // QB

    def kernel(*refs):
        ins, out, slab, sems = refs[:-3], refs[-3], refs[-2], refs[-1]
        copies = []
        for k, (d, n, _, part) in enumerate(entries):
            rows = part.shape[0]
            to = slab.at[pl.ds(n * rows, rows), pl.ds(slots.index(d) * wide, wide)]
            copies.append(pltpu.make_async_copy(ins[k], to, sems.at[k]))
        for copy in copies:
            copy.start()
        for copy in copies:
            copy.wait()
        for i in range(count):
            strip = contract(slab[i * QB : (i + 1) * QB], slab[i * QB :], 1, 1)
            for j in range(i, count):
                out[upper(count).index((i, j))] = strip[:, (j - i) * QB : (j - i + 1) * QB]

    return pl.pallas_call(
        kernel,
        in_specs=[pl.BlockSpec(memory_space=pl.ANY)] * len(entries),
        out_specs=pl.BlockSpec(memory_space=pltpu.VMEM),
        out_shape=jax.ShapeDtypeStruct((count * (count + 1) // 2, QB, QB), F32),
        scratch_shapes=[
            pltpu.VMEM((size, wide * len(slots)), BF),
            pltpu.SemaphoreType.DMA((len(entries),)),
        ],
        cost_estimate=pl.CostEstimate(
            flops=2 * size * size * wide * len(slots), transcendentals=0, bytes_accessed=2 * size * wide * len(slots)
        ),
        name="gram",
    )(*[part for _, _, _, part in entries])


def ortho_kernel(flag_ref, ga_ref, gb_ref, s_ref, out_ref, x_ref, gh, gl, th, tl, pm):
    size = gh.shape[0]
    count = size // QB
    parts = [slice(i * QB, (i + 1) * QB) for i in range(count)]
    pairs = upper(count)
    trace = jnp.zeros((), F32)
    row = lax.broadcasted_iota(jnp.int32, (QB, QB), 0)
    col = lax.broadcasted_iota(jnp.int32, (QB, QB), 1)
    for i in range(count):
        n = pairs.index((i, i))
        trace = trace + jnp.sum(jnp.where(row == col, ga_ref[n] + gb_ref[n], 0.0))
    scale = 1.0 / (jnp.sqrt(jnp.broadcast_to(trace, (1, 1))) + 1e-07)

    def put(i, j, block):
        high, low = split(block)
        gh[parts[i], parts[j]], gl[parts[i], parts[j]] = high, low
        if i != j:
            turned = block.T
            high, low = split(turned)
            gh[parts[j], parts[i]], gl[parts[j], parts[i]] = high, low

    for n, (i, j) in enumerate(pairs):
        put(i, j, (ga_ref[n] + gb_ref[n]) * (scale * scale))
    x_ref[...] = (s_ref[...].astype(F32) * scale).astype(BF)

    def poly():
        for i in range(count):
            rest = slice(i * QB, size)
            square = contract(gh[parts[i]], gh[:, rest], 1, 0)
            block = COEF_B * gh[parts[i], rest].astype(F32) + COEF_C * square
            pm[parts[i], rest] = block.astype(BF)
            for j in range(i + 1, count):
                pm[parts[j], parts[i]] = block[:, (j - i) * QB : (j - i + 1) * QB].T.astype(BF)

    def advance():
        x = x_ref[...]
        x_ref[...] = (COEF_A * x.astype(F32) + contract(pm[...], x, 1, 0)).astype(BF)

    def body(_, carry):
        poly()
        advance()
        for part in parts:
            left = pm[part]
            total = COEF_A * (gh[part].astype(F32) + gl[part].astype(F32))
            total = total + contract(left, gh[...], 1, 0) + contract(left, gl[...], 1, 0)
            th[part], tl[part] = split(total)
        for i in range(count):
            rest = slice(i * QB, size)
            total = COEF_A * (th[parts[i], rest].astype(F32) + tl[parts[i], rest].astype(F32))
            total = total + contract(th[parts[i]], pm[:, rest], 1, 0) + contract(tl[parts[i]], pm[:, rest], 1, 0)
            for j in range(i, count):
                put(i, j, total[:, (j - i) * QB : (j - i + 1) * QB])
        return carry

    lax.fori_loop(0, NS - 1, body, 0)
    poly()
    advance()
    nf, wide, _ = out_ref.shape
    unit = x_ref.shape[1] // nf

    @pl.when(flag_ref[0] == 0)
    def _():
        for a in range(nf):
            out_ref[a] = x_ref[a * wide : (a + 1) * wide]

    @pl.when(flag_ref[0] == 1)
    def _():
        for a in range(nf):
            for b in range(nf):
                out_ref[b, :, a * unit : (a + 1) * unit] = x_ref[a * wide : (a + 1) * wide, b * unit : (b + 1) * unit]


def orthogonalize(swapped, gram_a, gram_b, cols, nf):
    size = cols.shape[0]
    square = pltpu.VMEM((size, size), BF)
    vmem = pl.BlockSpec(memory_space=pltpu.VMEM)
    return pl.pallas_call(
        ortho_kernel,
        in_specs=[pl.BlockSpec(memory_space=pltpu.SMEM), vmem, vmem, vmem],
        out_specs=vmem,
        out_shape=jax.ShapeDtypeStruct((nf, size // nf, cols.shape[1]), BF),
        scratch_shapes=[pltpu.VMEM(cols.shape, BF)] + [square] * 5,
        cost_estimate=pl.CostEstimate(
            flops=40 * size**3, transcendentals=0, bytes_accessed=8 * size * size
        ),
        name="orthogonalize",
    )(swapped.astype(jnp.int32).reshape(1), gram_a, gram_b, cols)


def momentum_cols(active, moment, grads):
    nf, size, unit = grads.shape

    def kernel(flag_ref, m_ref, g_ref, out_ref):
        keep = jnp.full((size, unit), flag_ref[0], jnp.int32) == 1
        for b in range(nf):
            lanes = slice(b * unit, (b + 1) * unit)
            total = m_ref[:, lanes].astype(F32) + g_ref[b].astype(F32)
            out_ref[:, lanes] = jnp.where(keep, total, 0.0).astype(BF)

    vmem = pl.BlockSpec(memory_space=pltpu.VMEM)
    return pl.pallas_call(
        kernel,
        in_specs=[pl.BlockSpec(memory_space=pltpu.SMEM), vmem, vmem],
        out_specs=vmem,
        out_shape=jax.ShapeDtypeStruct(moment.shape, BF),
        name="momentum_cols",
    )(active.astype(jnp.int32).reshape(1), moment, grads)


def rep_scalar():
    return lax.axis_index("rep").astype(jnp.int32).reshape(1)


def assemble(pieces, nr):
    entries = listed(pieces)
    count = sum(part.shape[0] for part in pieces[0])
    tail = pieces[0][0].shape[1:]

    def kernel(r_ref, *refs):
        ins, out, sems = refs[:-2], refs[-2], refs[-1]
        copies = []
        for k, (d, n, _, part) in enumerate(entries):
            to = out.at[pl.ds(n * part.shape[0], part.shape[0]), r_ref[0] ^ d]
            copies.append(pltpu.make_async_copy(ins[k], to, sems.at[k]))
        for copy in copies:
            copy.start()
        for copy in copies:
            copy.wait()

    return pl.pallas_call(
        kernel,
        in_specs=[pl.BlockSpec(memory_space=pltpu.SMEM)] + [pl.BlockSpec(memory_space=pl.ANY)] * len(entries),
        out_specs=pl.BlockSpec(memory_space=pltpu.VMEM),
        out_shape=jax.ShapeDtypeStruct((count, nr) + tail, pieces[0][0].dtype),
        scratch_shapes=[pltpu.SemaphoreType.DMA((len(entries),))],
    )(rep_scalar(), *[part for _, _, _, part in entries])


def grad_mlp(which, d_pre, normed, hidden, cot, blocks, dtype):
    length, width = normed.shape
    mid = d_pre.shape[1] // 2
    step = min(mid, QB)
    count = mid // step
    unit = mid // blocks

    def kernel(w_ref, a_ref, x_ref, b_ref, y_ref, out_ref):
        def put(left, right):
            out_ref[0] = contract(left[...], right[...], 0, 0).reshape(step // unit, unit, width).astype(dtype)

        @pl.when(pl.program_id(0) == 0)
        def _():
            put(a_ref, x_ref)

        @pl.when(pl.program_id(0) == 1)
        def _():
            put(b_ref, y_ref)

    whole = pl.BlockSpec((length, width), lambda m, i, w: (0, 0))
    return pl.pallas_call(
        kernel,
        grid_spec=pltpu.PrefetchScalarGridSpec(
            num_scalar_prefetch=1,
            grid=(2, count),
            in_specs=[
                pl.BlockSpec((length, step), lambda m, i, w: (0, w[0] * count + jnp.where(m == 0, i, count - 1))),
                whole,
                pl.BlockSpec((length, step), lambda m, i, w: (0, w[0] * count + jnp.where(m == 1, i, 0))),
                whole,
            ],
            out_specs=pl.BlockSpec((1, step // unit, unit, width), lambda m, i, w: (m, i, 0, 0)),
        ),
        out_shape=jax.ShapeDtypeStruct((2, blocks, unit, width), dtype),
        cost_estimate=pl.CostEstimate(
            flops=4 * length * mid * width, transcendentals=0, bytes_accessed=8 * length * width
        ),
        name="grad_mlp",
    )(which.astype(jnp.int32).reshape(1), d_pre, normed, hidden, cot)


def grad_comb(which, dq, dk, dv, mixed, normed, cot, blocks, dtype):
    length, width = normed.shape
    step = dq.shape[1]
    unit = 2 * step // blocks

    def kernel(w_ref, q_ref, k_ref, v_ref, m_ref, x_ref, y_ref, out_ref):
        def put(left, right):
            out_ref[...] = contract(left[...], right[...], 0, 0).reshape(step // unit, unit, width).astype(dtype)

        at = 2 * w_ref[0] + pl.program_id(0)
        for n, (left, right) in enumerate(((q_ref, x_ref), (k_ref, x_ref), (v_ref, x_ref), (m_ref, y_ref))):

            @pl.when(at == n)
            def _(left=left, right=right):
                put(left, right)

    left = pl.BlockSpec((length, step), lambda i, w: (0, 0))
    whole = pl.BlockSpec((length, width), lambda i, w: (0, 0))
    return pl.pallas_call(
        kernel,
        grid_spec=pltpu.PrefetchScalarGridSpec(
            num_scalar_prefetch=1,
            grid=(2,),
            in_specs=[left] * 4 + [whole] * 2,
            out_specs=pl.BlockSpec((step // unit, unit, width), lambda i, w: (i, 0, 0)),
        ),
        out_shape=jax.ShapeDtypeStruct((blocks, unit, width), dtype),
        cost_estimate=pl.CostEstimate(
            flops=4 * length * step * width, transcendentals=0, bytes_accessed=8 * length * width
        ),
        name="grad_comb",
    )(which.astype(jnp.int32).reshape(1), dq, dk, dv, mixed, normed, cot)


def grad_rule(block, have):
    return block, MOMENTUM_RATE * have + block


def weight_rule(step):
    def rule(block, have):
        return (have.astype(F32) - step * block,)

    return rule


def finish_plain(pieces, have, rules, nr):
    whole = jnp.stack([jnp.concatenate(pieces[d], axis=1) for d in sorted(pieces)])
    index = jnp.arange(nr)
    source = (index // (nr // 2)) | ((index % (nr // 2)) << 1)
    whole = whole[source ^ lax.axis_index("rep")]
    per = nr // 4
    rows = whole.shape[2]
    nf = have[1].shape[1] // rows
    whole = whole.reshape(nr, 3, rows, nf, -1)
    unit = whole.shape[4]
    qkv = whole[: 3 * per, 0].reshape(3, per, rows, nf, unit).transpose(2, 0, 3, 1, 4).reshape(rows, -1)
    out = whole[3 * per :, 0].transpose(0, 3, 2, 1).reshape(rows, -1)
    up = whole[:, 1].transpose(1, 2, 0, 3).reshape(rows, -1)
    down = whole[:, 2].transpose(1, 2, 0, 3).reshape(rows, -1)
    return [rule(m.astype(F32), x) for m, x, rule in zip((qkv, out, up, down), have, rules)]


def finish(pieces, have, rules, outs, nr):
    entries = listed(pieces)
    parts = [part for _, _, _, part in entries]
    wide = parts[0].shape[2]
    rows = sum(part.shape[1] for part in pieces[0])
    nf = have[1].shape[1] // rows
    u = wide // nf
    if u % 128:
        return finish_plain(pieces, have, rules, nr)
    per = nr // 4
    order = [(2, 1, nf), (3, 2, nf), (0, 0, 3), (1, 0, 1)]
    starts = [0, nf, 2 * nf, 2 * nf + 3]
    steps = 2 * nf + 4

    def kernel(r_ref, *refs):
        ins = refs[: len(parts)]
        have_refs = refs[len(parts) : len(parts) + 4]
        out_refs = refs[len(parts) + 4 : len(parts) + 4 + 4 * outs]
        slab, sems = refs[-2:]
        step = pl.program_id(0)

        def copies(which):
            for k, (d, n, _, part) in enumerate(entries):
                to = slab.at[place(r_ref[0] ^ d, nr), which, pl.ds(n * part.shape[1], part.shape[1])]
                yield pltpu.make_async_copy(ins[k].at[which], to, sems.at[k, which])

        @pl.when(step == 0)
        def _():
            for which in (1, 2, 0):
                for copy in copies(which):
                    copy.start()

        def write(matrix, at, block):
            values = rules[matrix](block.astype(F32), have_refs[matrix][at])
            for n, value in enumerate(values):
                out_refs[matrix * outs + n][at] = value

        for (matrix, which, count), start in zip(order, starts):
            for k in range(count):

                @pl.when(step == start + k)
                def _(matrix=matrix, which=which, start=start, k=k):
                    if k == 0 and matrix != 1:
                        for copy in copies(which):
                            copy.wait()
                    if matrix >= 2:
                        for p in range(nr):
                            at = (slice(None), slice(p * u, (p + 1) * u))
                            write(matrix, at, slab[p, which, :, k * u : (k + 1) * u])
                    elif matrix == 0:
                        for b in range(nf):
                            for s in range(per):
                                at = (slice(None), slice((b * per + s) * u, (b * per + s + 1) * u))
                                write(0, at, slab[k * per + s, 0, :, b * u : (b + 1) * u])
                    else:
                        for b in range(nf):
                            for s in range(per):
                                at = (slice(s * u, (s + 1) * u), slice(b * rows, (b + 1) * rows))
                                write(1, at, slab[3 * per + s, 0, :, b * u : (b + 1) * u].astype(F32).T)

    specs = [None] * 4
    for (matrix, _, count), start in zip(order, starts):
        specs[matrix] = pl.BlockSpec(
            (rows, have[matrix].shape[1] // count),
            lambda i, start=start, count=count: (0, jnp.clip(i - start, 0, count - 1)),
        )
    shapes = [jax.ShapeDtypeStruct(m.shape, F32) for m in have for _ in range(outs)]
    flat = pl.pallas_call(
        kernel,
        grid=(steps,),
        in_specs=[pl.BlockSpec(memory_space=pltpu.SMEM)] + [pl.BlockSpec(memory_space=pl.ANY)] * len(parts) + specs,
        out_specs=[spec for spec in specs for _ in range(outs)],
        out_shape=shapes,
        scratch_shapes=[
            pltpu.VMEM((nr, 3, rows, wide), BF),
            pltpu.SemaphoreType.DMA((len(parts), 3)),
        ],
        cost_estimate=pl.CostEstimate(
            flops=rows * rows * 100, transcendentals=0, bytes_accessed=(6 + 4 * outs) * sum(m.size for m in have)
        ),
    )(rep_scalar(), *parts, *have)
    return [tuple(flat[m * outs : (m + 1) * outs]) for m in range(4)]


def layer_norm_parts(values):
    center = values - jnp.mean(values, axis=-1, keepdims=True)
    spread = jnp.mean(center * center, axis=-1, keepdims=True)
    scale = lax.rsqrt(spread + 1e-05)
    return center * scale, scale


def gelu_tanh(values):
    return jax.nn.gelu(values, approximate=True)


def on_device(
    tokens,
    cotangent,
    qkv_weight,
    out_weight,
    up_weight,
    down_weight,
    ln_gain,
    ln_bias,
    up_bias,
    down_bias,
    qkv_moment,
    out_moment,
    up_moment,
    down_moment,
    gain_moment,
    beta_moment,
    up_bias_moment,
    down_bias_moment,
):
    nf = lax.axis_size("fsdp")
    nr = lax.axis_size("rep")
    f = lax.axis_index("fsdp")
    r = lax.axis_index("rep")
    _, local_len, width = tokens.shape
    rows = qkv_weight.shape[0]
    hidden_width = up_weight.shape[1] // nf
    head_width = width // nf
    unit = hidden_width // nr
    qkv_units = 3 * nr // 4

    tok = tokens.reshape(local_len, width)
    cot = cotangent.reshape(local_len, width)

    share = rows // nr
    core = rep_bit(0)
    spot = place(r, nr)
    is_out = spot >= qkv_units
    out_plane = is_out & (f == 1)

    def by_dest(weight, thirds):
        part = lax.dynamic_slice_in_dim(weight, r * share, share, 0)
        step = weight.shape[1] // thirds
        wide = step // nf
        return [
            jnp.concatenate([part[:, t * step + b * wide : t * step + (b + 1) * wide] for t in range(thirds)], axis=1)
            for b in range(nf)
        ]

    def slab_of(got):
        pieces = with_partner(plane_pieces(got, 0, nr), nr)
        return assemble(pieces, nr).reshape(width, got.shape[2])

    vectors = jnp.concatenate([ln_gain, ln_bias, down_bias]).reshape(1, 3 * rows)
    vectors = jnp.concatenate([vectors, jnp.zeros((7, 3 * rows), BF)], axis=0)
    got = z_exchange(jnp.stack([jnp.concatenate([w, vectors], axis=0) for w in by_dest(qkv_weight, 3)]))
    vectors = got[:, share].astype(F32)
    gain, beta, down_bias_full = [vectors[:, i * rows : (i + 1) * rows].reshape(width) for i in range(3)]
    qkv_cols = slab_of(got[:, :share])

    mlp = [jnp.concatenate(p, axis=1) for p in zip(by_dest(up_weight, 1), by_dest(down_weight, 1))]
    mlp = z_exchange(after(jnp.stack(mlp), got))
    mlp = slab_of(mlp)
    tok_near = z_neighbours(tok, nf)
    cot_near = z_neighbours(after(cot, *tok_near), nf)
    tok_all = z_gather(tok, tok_near, nf)
    length = tok_all.shape[0]
    cot_near = lax.optimization_barrier((*cot_near, tok_all))[:2]
    cot_all = z_gather(cot, cot_near, nf)
    up_cols, down_cols = mlp[:, :hidden_width], mlp[:, hidden_width:]

    xhat_all, _ = layer_norm_parts(tok_all.astype(F32))
    normed = (xhat_all * gain + beta).astype(BF)
    projected = jnp.dot(normed, qkv_cols, preferred_element_type=F32)
    tables = rotary_tables(length)
    q, k, v, probs, mixed = attend(projected, tables, head_width)
    hidden_pre = jnp.dot(normed, up_cols, preferred_element_type=F32) + up_bias.astype(F32)
    hidden_f, gelu_pull = jax.vjp(gelu_tanh, hidden_pre)
    hidden = hidden_f.astype(BF)

    def unit_columns(moment, thirds):
        step = moment.shape[1] // thirds
        wide = step // nf
        inside = jnp.minimum(spot, thirds * wide // unit - 1) * unit
        start = (inside // wide) * step + inside % wide
        parts = [lax.dynamic_slice_in_dim(moment, start + b * wide, unit, 1) for b in range(nf)]
        return jnp.concatenate(parts, axis=1)

    def side_by_side(blocks):
        return jnp.concatenate([blocks[b] for b in range(nf)], axis=1)

    held = lax.optimization_barrier((qkv_moment, out_moment, up_moment, down_moment, normed))[:4]
    out_start = jnp.maximum(spot - qkv_units, 0) * unit
    out_rows = lax.dynamic_slice_in_dim(held[1], out_start, unit, 0).T
    out_rows = side_by_side(out_rows.reshape(nf, rows, unit))
    owned = [unit_columns(held[0], 3), out_rows, unit_columns(held[2], 1), unit_columns(held[3], 1)]
    owned = [(MOMENTUM_RATE * m).astype(BF) for m in owned]
    owned = owned + [jnp.zeros((rows, nf * unit), BF)] * (nf - 4)
    moment_in = z_exchange(after(jnp.stack(owned), cot_all))
    moment_out = [side_by_side(moment_in[:, :, b * unit : (b + 1) * unit]) for b in range(nf)]
    moment_cols = jnp.where(out_plane, jnp.concatenate(moment_out, axis=0), moment_in.reshape(width, nf * unit))

    d_hidden = jnp.dot(cot_all, down_cols, preferred_element_type=F32)
    d_pre = gelu_pull(d_hidden)[0].astype(BF)
    lanes = nr // 2

    def joined(mine, other):
        return mine + xor_swap(other, 1, nr).astype(F32)

    order = high_bits(nr)
    mlp_parts = (d_pre, normed, hidden, cot_all, lanes)
    sum_mlp = joined(grad_mlp(core, *mlp_parts, F32), grad_mlp(1 - core, *mlp_parts, BF))
    unit_up, unit_down = plane_sum(sum_mlp[0], order, nr), plane_sum(sum_mlp[1], order[::-1], nr)

    d_mixed = contract(cot_all, out_weight, 1, 1).astype(BF)
    dq, dk, dv = attend_back(q, k, v, probs, d_mixed, tables)
    comb_parts = (dq, dk, dv, mixed, normed, cot_all, lanes)
    sum_comb = joined(grad_comb(core, *comb_parts, F32), grad_comb(1 - core, *comb_parts, BF))
    unit_comb = jnp.concatenate(
        [
            plane_sum(sum_comb[:, : unit // 2], order, nr),
            plane_sum(sum_comb[:, unit // 2 :], order[::-1], nr),
        ],
        axis=0,
    )

    partial_out = jnp.dot(mixed, out_weight, preferred_element_type=F32) + contract(hidden, down_cols, 1, 1)
    partial_out = partial_out.astype(BF).reshape(nf, local_len, width)
    summed = z_exchange(after(partial_out, moment_in))

    units = [u.astype(BF).T for u in (unit_comb, unit_up, unit_down)]
    sends = [units[0], units[0], units[1], units[2]] + [jnp.zeros((width, unit), BF)] * (nf - 4)
    grad_cols = z_exchange(after(jnp.stack(sends), summed))
    active = jnp.where(f == 0, ~is_out, jnp.where(f == 1, is_out, f < 4))
    s_cols = momentum_cols(active, moment_cols, grad_cols)

    s_pieces = plane_pieces(s_cols, 0, nr)
    gram = gram_of(s_pieces)
    gram_other = xor_swap(gram, 1, nr)

    grad_send = jnp.stack([jnp.stack([u[b * rows : (b + 1) * rows] for b in range(nf)]) for u in units], axis=1)
    grad_got = z_exchange(after(grad_send, grad_cols))
    kept = jnp.where(is_out, grad_send[:, 0], grad_got[:, 0])
    grad_mine = [side_by_side(g) for g in (kept, grad_got[:, 1], grad_got[:, 2])]
    grad_mine = after(jnp.stack(grad_mine), *[part for d in sorted(s_pieces) for part in s_pieces[d]])
    grad_pieces = {0: (grad_mine,)}
    for mask in range(2, nr, 2):
        grad_pieces[mask] = (xor_swap(grad_mine, mask, nr),)

    d_projected = jnp.concatenate([after(dq, grad_cols), dk, dv], axis=1)
    partial_normed = contract(d_projected, qkv_cols, 1, 1) + contract(d_pre, up_cols, 1, 1)
    partial_normed = partial_normed.astype(BF).reshape(nf, local_len, width)
    summed_normed = z_exchange(after(partial_normed, grad_got))

    ortho = orthogonalize(out_plane, gram, gram_other, s_cols, nf)
    back = z_exchange(after(ortho, summed_normed))
    ortho_mine = jnp.stack([jnp.where(is_out, back[1], back[0]), back[2], back[3]])
    ortho_pieces = with_partner(plane_pieces(ortho_mine, 1, nr), nr)

    mats = (qkv_weight, out_weight, up_weight, down_weight)
    moments = (qkv_moment, out_moment, up_moment, down_moment)
    done = finish(with_partner(grad_pieces, nr), moments, [grad_rule] * 4, 2, nr)
    grads, new_moments = [d[0] for d in done], [d[1] for d in done]
    rules = [weight_rule(MATRIX_RATE * 0.2 * math.sqrt(w.shape[1])) for w in mats]
    new_mats = [d[0] for d in finish(ortho_pieces, mats, rules, 1, nr)]

    inputs = tok.astype(F32)
    block_out = (inputs + jnp.sum(summed.astype(F32), axis=0) + down_bias_full).astype(BF)
    d_normed = jnp.sum(summed_normed.astype(F32), axis=0)
    xhat, inv_std = layer_norm_parts(inputs)
    e = d_normed * gain
    input_grad = cot.astype(F32) + inv_std * (
        e - jnp.mean(e, axis=-1, keepdims=True) - xhat * jnp.mean(e * xhat, axis=-1, keepdims=True)
    )

    pair = jnp.stack([jnp.sum(d_normed * xhat, axis=0), jnp.sum(d_normed, axis=0)])
    pair = pair.reshape(2, nf, rows).transpose(1, 0, 2)
    pair = jnp.sum(z_exchange(after(pair, back)), axis=0).reshape(2 * rows)
    down_sum = jnp.sum(lax.dynamic_slice_in_dim(cot_all, f * rows, rows, 1).astype(F32), axis=0)
    up_sum = jnp.sum(d_pre.astype(F32), axis=0)
    small = plane_sum_small(jnp.concatenate([pair, down_sum, up_sum]), nr)
    vec_grads = [small[:rows], small[rows : 2 * rows], small[3 * rows :], small[2 * rows : 3 * rows]]
    vec_moments = [
        MOMENTUM_RATE * m + g
        for m, g in zip((gain_moment, beta_moment, up_bias_moment, down_bias_moment), vec_grads)
    ]
    vec_new = [
        p.astype(F32) - VECTOR_RATE * m for p, m in zip((ln_gain, ln_bias, up_bias, down_bias), vec_moments)
    ]

    return (
        block_out.reshape(1, local_len, width),
        input_grad.reshape(1, local_len, width),
        *grads,
        *vec_grads,
        *new_mats,
        *vec_new,
        *new_moments,
        *vec_moments,
    )


def solution(mesh):
    split3 = P("rep", "fsdp", None)
    mat = P("fsdp", None)
    vec = P("fsdp")

    return jax.shard_map(
        on_device,
        mesh=mesh,
        in_specs=(split3,) * 2 + (mat,) * 4 + (vec,) * 4 + (mat,) * 4 + (vec,) * 4,
        out_specs=(split3,) * 2 + ((mat,) * 4 + (vec,) * 4) * 3,
        check_vma=False,
    )
```

profile of v0, /device:TPU:0, one launch (start us, length us, event | category | flops | bytes accessed | tf_op | source)
XLA Modules:
  0.0 583.7 jit_solution(2505127110553535139)
XLA Ops:
  2.0 5.6 collective-permute-start
  19.0 5.2 all-to-all-done
  41.1 7.5 %all-to-all-start.1 = ((bf16[4,32,2048]{2,1,0:T(8,128)(2,1)}), bf16[4,32,2048]{2,1,0:T(8,128)(2,1)}, u32[]{:S(2)}, u32[]{:S(2)}) async-start(bf16[4,32,2048]{2,1,0:T(8,128)(2,1)} %pad_maximum_fusion.5), calls=%async_computation.1 | async-start | bytes 1048576 | tf_op jit(solution)/shard_map/all_to_all | solution.py:56
  49.9 5.4 collective-permute-start.24
  60.9 32.4 %collective-permute-done.4 = bf16[256,1024]{1,0:T(8,128)(2,1)S(1)} collective-permute-done((bf16[256,1024]{1,0:T(8,128)(2,1)S(1)}, bf16[256,1024]{1,0:T(8,128)(2,1)S(1)}, u32[]{:S(2)}, u32[]{:S(2)}) %collective-permute-start.4) | collective-permute-done | bytes 524320 | tf_op jit(solution)/shard_map/ppermute | solution.py:50
  105.0 4.9 fusion.82.qf_ref.kf_ref.vf_ref
  114.4 14.0 %attend.1 = (bf16[1024,256]{1,0:T(8,128)(2,1)}, bf16[1024,256]{1,0:T(8,128)(2,1)}, bf16[1024,256]{1,0:T(8,128)(2,1)}, bf16[4,1024,1024]{2,1,0:T(8,128)(2,1)}, bf16[1024,256]{1,0:T(8,128)(2,1)}) custom-call(f32[1024,768]{1,0:T(8,128)} %fusion.82.qf_ref.kf_ref.vf_ref, f32[1024,768]{1,0:T(8,128)} %fusion.82.qf_ref.kf_ref.vf_ref, ...), custom_call_target="tpu_custom_call" | custom-call | tf_op jit(solution)/shard_map/attend/pallas_call | solution.py:180
  139.9 5.5 collective-permute-done.18.refs_4_
  156.5 10.8 %all-to-all-start.2 = ((bf16[4,256,512]{2,1,0:T(8,128)(2,1)}), bf16[4,256,512]{2,1,0:T(8,128)(2,1)S(1)}, u32[]{:S(2)}, u32[]{:S(2)}) async-start(bf16[4,256,512]{2,1,0:T(8,128)(2,1)} %pad_maximum_fusion), calls=%async_computation.2 | async-start | bytes 2097152 | tf_op jit(solution)/shard_map/all_to_all | solution.py:56
  167.3 17.5 %attend_back.1 = (bf16[1024,256]{1,0:T(8,128)(2,1)}, bf16[1024,256]{1,0:T(8,128)(2,1)}, bf16[1024,256]{1,0:T(8,128)(2,1)}) custom-call(bf16[1024,256]{1,0:T(8,128)(2,1)} %get-tuple-element.74.q_ref, bf16[1024,256]{1,0:T(8,128)(2,1)} %get-tuple-element.75.k_ref, bf16[1024,256]{1,0:T(8,128)(2,1)} %get-tuple-element.76.v_ref, ...), custom_call_target="tpu_custom_call" | custom-call | tf_op jit(solution)/shard_map/attend_back/pallas_call | solution.py:224
  184.8 5.2 grad_comb.3
  190.0 5.8 grad_comb.2
  200.6 6.2 %multiply_convert_fusion = (bf16[1024,1024]{1,0:T(8,128)(2,1)}, f32[1024,1024]{1,0:T(8,128)S(1)}) fusion(f32[1024]{0:T(1024)S(1)} %convert_element_type.235, bf16[1024,1024]{1,0:T(8,128)(2,1)S(1)} %copy-done.1, bf16[1024,2048]{1,0:T(8,128)(2,1)} %bitcast.267), kind=kOutput, calls=%fused_computation.24 | convolution fusion | flops 2157969408 | bytes 10489856 | tf_op jit(solution)/shard_map/dot_general | solution.py:695
  206.9 6.0 %convert_reduce_fusion.3 = (f32[1024]{0:T(1024)S(1)}, bf16[1024,1024]{1,0:T(8,128)(2,1)}) fusion(f32[1024,1024]{1,0:T(8,128)S(1)} %get-tuple-element.220, f32[1024]{0:T(1024)S(1)} %convert_element_type.235, bf16[1024,1024]{1,0:T(8,128)(2,1)S(1)} %copy-done.3, bf16[1024,2048]{1,0:T(8,128)(2,1)S(1)} %bitcast.270), kind=kOutput, calls=%fused_computation.19 | convolution fusion | flops 2171599872 | bytes 10493952 | tf_op jit(solution)/shard_map/dot_general | solution.py:721
  212.9 7.0 %grad_mlp.3 = bf16[2,4,128,1024]{3,2,1,0:T(8,128)(2,1)} custom-call(s32[1]{0:T(128)} %bitcast.33.w_ref, bf16[1024,1024]{1,0:T(8,128)(2,1)} %get-tuple-element.222.a_ref, bf16[1024,1024]{1,0:T(8,128)(2,1)} %copy-done, bf16[1024,1024]{1,0:T(8,128)(2,1)} %get-tuple-element.219.b_ref, bf16[1024,1024]{1,0:T(8,128)(2,1)} %copy-done.2), custom_call_target="tpu_custom_call" | custom-call | flops 2147483648 | bytes 8388608 | tf_op jit(solution)/shard_map/grad_mlp/pallas_call | solution.py:441
  220.2 6.7 %add_convert_fusion.1 = bf16[1024,1024]{1,0:T(8,128)(2,1)} fusion(f32[1024,1024]{1,0:T(8,128)} %fusion.83, bf16[1024,1024]{1,0:T(8,128)(2,1)S(1)} %copy-done.9, bf16[1024,2048]{1,0:T(8,128)(2,1)} %bitcast.268), kind=kOutput, calls=%fused_computation.23 | convolution fusion | flops 2149580800 | bytes 10485760 | tf_op jit(solution)/shard_map/dot_general | solution.py:28
  231.7 7.3 %grad_mlp.2 = f32[2,4,128,1024]{3,2,1,0:T(8,128)} custom-call(s32[1]{0:T(128)} %bitcast.32.w_ref, bf16[1024,1024]{1,0:T(8,128)(2,1)} %get-tuple-element.222.a_ref, bf16[1024,1024]{1,0:T(8,128)(2,1)} %copy-done, bf16[1024,1024]{1,0:T(8,128)(2,1)} %get-tuple-element.219.b_ref, bf16[1024,1024]{1,0:T(8,128)(2,1)} %copy-done.2), custom_call_target="tpu_custom_call" | custom-call | flops 2147483648 | bytes 8388608 | tf_op jit(solution)/shard_map/grad_mlp/pallas_call | solution.py:441
  247.6 9.5 %collective-permute-done.33 = bf16[2,64,1024]{1,2,0:T(8,128)(2,1)S(1)} collective-permute-done((bf16[2,64,1024]{1,2,0:T(8,128)(2,1)S(1)}, bf16[2,64,1024]{1,2,0:T(8,128)(2,1)S(1)}, u32[]{:S(2)}, u32[]{:S(2)}) %collective-permute-start.33) | collective-permute-done | bytes 262176 | tf_op jit(solution)/shard_map/ppermute | solution.py:60
  259.2 5.1 all-to-all-start.3
  291.6 5.4 collective-permute-done.38
  314.7 4.8 maximum_select_fusion.m_ref
  319.5 20.2 %all-to-all-done.4.g_ref = bf16[4,1024,128]{2,1,0:T(8,128)(2,1)} async-done(((bf16[4,1024,128]{2,1,0:T(8,128)(2,1)}), bf16[4,1024,128]{2,1,0:T(8,128)(2,1)}, u32[]{:S(2)}, u32[]{:S(2)}) %all-to-all-start.4) | async-done | bytes 1048608 | tf_op jit(solution)/shard_map/all_to_all | solution.py:56
  345.3 21.7 %collective-permute-done.41.refs_2_ = bf16[1024,512]{1,0:T(8,128)(2,1)S(1)} collective-permute-done((bf16[1024,512]{1,0:T(8,128)(2,1)}, bf16[1024,512]{1,0:T(8,128)(2,1)S(1)}, u32[]{:S(2)}, u32[]{:S(2)}) %collective-permute-start.41) | collective-permute-done | bytes 1048608 | tf_op jit(solution)/shard_map/ppermute | solution.py:60
  370.7 8.5 %collective-permute-done.42.refs_3_ = bf16[512,512]{1,0:T(8,128)(2,1)S(1)} collective-permute-done((bf16[512,512]{1,0:T(8,128)(2,1)S(1)}, bf16[512,512]{1,0:T(8,128)(2,1)S(1)}, u32[]{:S(2)}, u32[]{:S(2)}) %collective-permute-start.42) | collective-permute-done | bytes 524320 | tf_op jit(solution)/shard_map/ppermute | solution.py:60
  380.3 6.6 %gram.1.ga_ref = f32[10,256,256]{2,1,0:T(8,128)} custom-call(bf16[1024,512]{1,0:T(8,128)(2,1)} %momentum_cols.1.refs_0_.s_ref, bf16[1024,512]{1,0:T(8,128)(2,1)} %copy-done.43, bf16[1024,512]{1,0:T(8,128)(2,1)} %copy-done.42, bf16[512,512]{1,0:T(8,128)(2,1)} %copy-done.63, bf16[512,512]{1,0:T(8,128)(2,1)} %collective-permute-done.43.refs_4_), custom_call_target="tpu_custom_call" | custom-call | flops 4294967296 | bytes 4194304 | tf_op jit(solution)/shard_map/gram/pallas_call | solution.py:267
  399.0 13.6 %all-to-all-done.5 = bf16[4,3,256,128]{3,2,1,0:T(8,128)(2,1)S(1)} async-done(((bf16[4,3,256,128]{3,2,1,0:T(8,128)(2,1)}), bf16[4,3,256,128]{3,2,1,0:T(8,128)(2,1)S(1)}, u32[]{:S(2)}, u32[]{:S(2)}) %all-to-all-start.5) | async-done | bytes 786464 | tf_op jit(solution)/shard_map/all_to_all | solution.py:56
  418.7 49.2 %orthogonalize.1 = bf16[4,256,512]{2,1,0:T(8,128)(2,1)} custom-call(s32[1]{0:T(128)} %bitcast.114.flag_ref, f32[10,256,256]{2,1,0:T(8,128)} %gram.1.ga_ref, f32[10,256,256]{2,1,0:T(8,128)} %collective-permute-done.51.gb_ref, bf16[1024,512]{1,0:T(8,128)(2,1)} %momentum_cols.1.refs_0_.s_ref), custom_call_target="tpu_custom_call" | custom-call | flops 42949672960 | bytes 8388608 | tf_op jit(solution)/shard_map/orthogonalize/pallas_call | solution.py:359
  467.9 5.2 all-to-all-start.7
  478.4 17.4 %collective-permute-done.49.refs_6_ = bf16[3,256,512]{2,1,0:T(8,128)(2,1)} collective-permute-done((bf16[3,256,512]{2,1,0:T(8,128)(2,1)S(1)}, bf16[3,256,512]{2,1,0:T(8,128)(2,1)}, u32[]{:S(2)}, u32[]{:S(2)}) %collective-permute-start.49) | collective-permute-done | bytes 786464 | tf_op jit(solution)/shard_map/ppermute | solution.py:60
  495.8 14.9 %collective-permute-done.47.refs_4_ = bf16[3,256,512]{2,1,0:T(8,128)(2,1)} collective-permute-done((bf16[3,256,512]{2,1,0:T(8,128)(2,1)S(1)}, bf16[3,256,512]{2,1,0:T(8,128)(2,1)}, u32[]{:S(2)}, u32[]{:S(2)}) %collective-permute-start.47) | collective-permute-done | bytes 786464 | tf_op jit(solution)/shard_map/ppermute | solution.py:60
  529.6 19.4 %shard_map.379 = (f32[256,3072]{1,0:T(8,128)}, f32[256,3072]{1,0:T(8,128)}, f32[256,1024]{1,0:T(8,128)}, f32[256,1024]{1,0:T(8,128)}, f32[256,4096]{1,0:T(8,128)...) custom-call(s32[1]{0:T(128)} %bitcast.5.r_ref, bf16[3,256,512]{2,1,0:T(8,128)(2,1)} %copy-done.17, ...), custom_call_target="tpu_custom_call" | custom-call | flops 6553600 | bytes 44040192 | tf_op jit(solution)/shard_map/pallas_call | solution.py:591
  569.1 14.1 %shard_map.380 = (f32[256,3072]{1,0:T(8,128)}, f32[256,1024]{1,0:T(8,128)}, f32[256,4096]{1,0:T(8,128)}, f32[256,4096]{1,0:T(8,128)}) custom-call(s32[1]{0:T(128)} %bitcast.5.r_ref, bf16[3,256,512]{2,1,0:T(8,128)(2,1)} %pad_maximum_fusion.4.refs_0_, bf16[3,256,512]{2,1,0:T(8,128)(2,1)} %collective-permute-done.55.refs_1_, ...), custom_call_target="tpu_custom_call" | custom-call | flops 6553600 | bytes 31457280 | tf_op jit(solution)/shard_map/pallas_call | solution.py:591
  (396 shorter events, 212.5 us)
Async XLA Ops:
  0.7 33.9 %collective-permute-start.3 = (bf16[256,1024]{1,0:T(8,128)(2,1)}, bf16[256,1024]{1,0:T(8,128)(2,1)S(1)}, u32[]{:S(2)}, u32[]{:S(2)}) collective-permute-start(bf16[256,1024]{1,0:T(8,128)(2,1)} %bitcast.259), channel_id=1, source_target_pairs={{1,0},{2,1},{3,2},{5,4},{6,5},{7,6},{9,8},{10,9},{11,10},{13,12},{... | collective-permute-start | bytes 1572872 | tf_op jit(solution)/shard_map/ppermute | solution.py:39
  27.4 31.9 %collective-permute-start.1 = (bf16[256,1024]{1,0:T(8,128)(2,1)S(1)}, bf16[256,1024]{1,0:T(8,128)(2,1)S(1)}, u32[]{:S(2)}, u32[]{:S(2)}) collective-permute-start(bf16[256,1024]{1,0:T(8,128)(2,1)S(1)} %collective-permute-done), channel_id=1, source_target_pairs={{1,3},{5,7},{9,11},{13,15},{17,19},{21,23},{25,27},{29,31}} | collective-permute-start | bytes 1572872 | tf_op jit(solution)/shard_map/ppermute | solution.py:49
  33.0 27.7 %collective-permute-start.2 = (bf16[256,1024]{1,0:T(8,128)(2,1)S(1)}, bf16[256,1024]{1,0:T(8,128)(2,1)S(1)}, u32[]{:S(2)}, u32[]{:S(2)}) collective-permute-start(bf16[256,1024]{1,0:T(8,128)(2,1)S(1)} %collective-permute-done), channel_id=1, source_target_pairs={{1,2},{2,3},{5,6},{6,7},{9,10},{10,11},{13,14},{14,15},{17,18},{18... | collective-permute-start | bytes 1572872 | tf_op jit(solution)/shard_map/ppermute | solution.py:49
  41.1 91.1 %all-to-all-start.1 = ((bf16[4,32,2048]{2,1,0:T(8,128)(2,1)}), bf16[4,32,2048]{2,1,0:T(8,128)(2,1)}, u32[]{:S(2)}, u32[]{:S(2)}) async-start(bf16[4,32,2048]{2,1,0:T(8,128)(2,1)} %pad_maximum_fusion.5), calls=%async_computation.1 | async-start | bytes 1048576 | tf_op jit(solution)/shard_map/all_to_all | solution.py:56
  48.6 46.2 %collective-permute-start.25 = (bf16[256,1024]{1,0:T(8,128)(2,1)S(1)}, bf16[256,1024]{1,0:T(8,128)(2,1)}, u32[]{:S(2)}, u32[]{:S(2)}) collective-permute-start(bf16[256,1024]{1,0:T(8,128)(2,1)S(1)} %bitcast.279), channel_id=1, source_target_pairs={{1,0},{2,1},{3,2},{5,4},{6,5},{7,6},{9,8},{10,9},{11,10},{13,12},{... | collective-permute-start | bytes 1572872 | tf_op jit(solution)/shard_map/ppermute | solution.py:39
  49.9 44.9 %collective-permute-start.24 = (bf16[256,1024]{1,0:T(8,128)(2,1)S(1)}, bf16[256,1024]{1,0:T(8,128)(2,1)}, u32[]{:S(2)}, u32[]{:S(2)}) collective-permute-start(bf16[256,1024]{1,0:T(8,128)(2,1)S(1)} %bitcast.280), channel_id=1, source_target_pairs={{0,1},{1,2},{2,3},{4,5},{5,6},{6,7},{8,9},{9,10},{10,11},{12,13},{... | collective-permute-start | bytes 1572872 | tf_op jit(solution)/shard_map/ppermute | solution.py:38
  55.3 38.1 %collective-permute-start.5 = (bf16[256,1024]{1,0:T(8,128)(2,1)S(1)}, bf16[256,1024]{1,0:T(8,128)(2,1)}, u32[]{:S(2)}, u32[]{:S(2)}) collective-permute-start(bf16[256,1024]{1,0:T(8,128)(2,1)S(1)} %collective-permute-done.3), channel_id=1, source_target_pairs={{2,0},{6,4},{10,8},{14,12},{18,16},{22,20},{26,24},{30,28}} | collective-permute-start | bytes 1572872 | tf_op jit(solution)/shard_map/ppermute | solution.py:50
  59.3 34.0 %collective-permute-start.4 = (bf16[256,1024]{1,0:T(8,128)(2,1)S(1)}, bf16[256,1024]{1,0:T(8,128)(2,1)S(1)}, u32[]{:S(2)}, u32[]{:S(2)}) collective-permute-start(bf16[256,1024]{1,0:T(8,128)(2,1)S(1)} %collective-permute-done.3), channel_id=1, source_target_pairs={{1,0},{2,1},{5,4},{6,5},{9,8},{10,9},{13,12},{14,13},{17,16},{18,1... | collective-permute-start | bytes 1572872 | tf_op jit(solution)/shard_map/ppermute | solution.py:50
  94.8 40.6 %collective-permute-start.27 = (bf16[256,1024]{1,0:T(8,128)(2,1)}, bf16[256,1024]{1,0:T(8,128)(2,1)}, u32[]{:S(2)}, u32[]{:S(2)}) collective-permute-start(bf16[256,1024]{1,0:T(8,128)(2,1)} %collective-permute-done.24), channel_id=1, source_target_pairs={{1,2},{2,3},{5,6},{6,7},{9,10},{10,11},{13,14},{14,15},{17,18},{18... | collective-permute-start | bytes 1572872 | tf_op jit(solution)/shard_map/ppermute | solution.py:49
  96.5 37.3 %collective-permute-start.26 = (bf16[256,1024]{1,0:T(8,128)(2,1)}, bf16[256,1024]{1,0:T(8,128)(2,1)}, u32[]{:S(2)}, u32[]{:S(2)}) collective-permute-start(bf16[256,1024]{1,0:T(8,128)(2,1)} %collective-permute-done.24), channel_id=1, source_target_pairs={{1,3},{5,7},{9,11},{13,15},{17,19},{21,23},{25,27},{29,31}} | collective-permute-start | bytes 1572872 | tf_op jit(solution)/shard_map/ppermute | solution.py:49
  97.9 51.5 %collective-permute-start.29 = (bf16[256,1024]{1,0:T(8,128)(2,1)}, bf16[256,1024]{1,0:T(8,128)(2,1)}, u32[]{:S(2)}, u32[]{:S(2)}) collective-permute-start(bf16[256,1024]{1,0:T(8,128)(2,1)} %collective-permute-done.25), channel_id=1, source_target_pairs={{2,0},{6,4},{10,8},{14,12},{18,16},{22,20},{26,24},{30,28}} | collective-permute-start | bytes 1572872 | tf_op jit(solution)/shard_map/ppermute | solution.py:50
  99.2 39.6 %collective-permute-start.28 = (bf16[256,1024]{1,0:T(8,128)(2,1)}, bf16[256,1024]{1,0:T(8,128)(2,1)}, u32[]{:S(2)}, u32[]{:S(2)}) collective-permute-start(bf16[256,1024]{1,0:T(8,128)(2,1)} %collective-permute-done.25), channel_id=1, source_target_pairs={{1,0},{2,1},{5,4},{6,5},{9,8},{10,9},{13,12},{14,13},{17,16},{18,1... | collective-permute-start | bytes 1572872 | tf_op jit(solution)/shard_map/ppermute | solution.py:50
  135.4 60.5 %collective-permute-start.15 = (bf16[4,32,2048]{2,1,0:T(8,128)(2,1)}, bf16[4,32,2048]{2,1,0:T(8,128)(2,1)}, u32[]{:S(2)}, u32[]{:S(2)}) collective-permute-start(bf16[4,32,2048]{2,1,0:T(8,128)(2,1)} %all-to-all-done.1.refs_0_), channel_id=1, source_target_pairs={{0,4},{4,0},{8,12},{12,8},{16,20},{20,16},{24,28},{28,24},{1,5},{5... | collective-permute-start | bytes 1572872 | tf_op jit(solution)/shard_map/ppermute | solution.py:60
  150.5 45.6 %collective-permute-start.19 = (bf16[4,32,2048]{2,1,0:T(8,128)(2,1)}, bf16[4,32,2048]{2,1,0:T(8,128)(2,1)}, u32[]{:S(2)}, u32[]{:S(2)}) collective-permute-start(bf16[4,32,2048]{2,1,0:T(8,128)(2,1)} %collective-permute-done.18.refs_4_), channel_id=1, source_target_pairs={{0,4},{4,0},{8,12},{12,8},{16,20},{20,16},{24,28},{28,24},{1,5},{5... | collective-permute-start | bytes 1572872 | tf_op jit(solution)/shard_map/ppermute | solution.py:60
  150.6 45.6 %collective-permute-start.17 = (bf16[4,32,2048]{2,1,0:T(8,128)(2,1)}, bf16[4,32,2048]{2,1,0:T(8,128)(2,1)}, u32[]{:S(2)}, u32[]{:S(2)}) collective-permute-start(bf16[4,32,2048]{2,1,0:T(8,128)(2,1)} %collective-permute-done.16.refs_2_), channel_id=1, source_target_pairs={{0,4},{4,0},{8,12},{12,8},{16,20},{20,16},{24,28},{28,24},{1,5},{5... | collective-permute-start | bytes 1572872 | tf_op jit(solution)/shard_map/ppermute | solution.py:60
  152.8 43.4 %collective-permute-start.22 = (bf16[2,32,2048]{2,1,0:T(8,128)(2,1)S(1)}, bf16[2,32,2048]{2,1,0:T(8,128)(2,1)}, u32[]{:S(2)}, u32[]{:S(2)}) collective-permute-start(bf16[2,32,2048]{2,1,0:T(8,128)(2,1)S(1)} %collective-permute-done.20.refs_6_), channel_id=1, source_target_pairs={{0,4},{4,0},{8,12},{12,8},{16,20},{20,16},{24,28},{28,24},{1,5},{5... | collective-permute-start | bytes 786440 | tf_op jit(solution)/shard_map/ppermute | solution.py:60
  155.0 41.2 %collective-permute-start.23 = (bf16[2,32,2048]{2,1,0:T(8,128)(2,1)}, bf16[2,32,2048]{2,1,0:T(8,128)(2,1)}, u32[]{:S(2)}, u32[]{:S(2)}) collective-permute-start(bf16[2,32,2048]{2,1,0:T(8,128)(2,1)} %collective-permute-done.21.refs_7_), channel_id=1, source_target_pairs={{0,4},{4,0},{8,12},{12,8},{16,20},{20,16},{24,28},{28,24},{1,5},{5... | collective-permute-start | bytes 786440 | tf_op jit(solution)/shard_map/ppermute | solution.py:60
  156.5 102.6 %all-to-all-start.2 = ((bf16[4,256,512]{2,1,0:T(8,128)(2,1)}), bf16[4,256,512]{2,1,0:T(8,128)(2,1)S(1)}, u32[]{:S(2)}, u32[]{:S(2)}) async-start(bf16[4,256,512]{2,1,0:T(8,128)(2,1)} %pad_maximum_fusion), calls=%async_computation.2 | async-start | bytes 2097152 | tf_op jit(solution)/shard_map/all_to_all | solution.py:56
  195.9 31.0 %collective-permute-start.30 = (bf16[4,128,1024]{2,1,0:T(8,128)(2,1)}, bf16[4,128,1024]{2,1,0:T(8,128)(2,1)}, u32[]{:S(2)}, u32[]{:S(2)}) collective-permute-start(bf16[4,128,1024]{2,1,0:T(8,128)(2,1)} %grad_comb.3), channel_id=1, source_target_pairs={{0,4},{4,0},{8,12},{12,8},{16,20},{20,16},{24,28},{28,24},{1,5},{5... | collective-permute-start | bytes 3145736 | tf_op jit(solution)/shard_map/ppermute | solution.py:60
  219.9 44.3 %collective-permute-start.35 = (bf16[2,4,128,1024]{3,2,1,0:T(8,128)(2,1)}, bf16[2,4,128,1024]{3,2,1,0:T(8,128)(2,1)}, u32[]{:S(2)}, u32[]{:S(2)}) collective-permute-start(bf16[2,4,128,1024]{3,2,1,0:T(8,128)(2,1)} %grad_mlp.3), channel_id=1, source_target_pairs={{0,4},{4,0},{8,12},{12,8},{16,20},{20,16},{24,28},{28,24},{1,5},{5... | collective-permute-start | bytes 6291464 | tf_op jit(solution)/shard_map/ppermute | solution.py:60
  246.4 28.5 %collective-permute-start.32 = (bf16[64,1024]{0,1:T(8,128)(2,1)S(1)}, bf16[64,1024]{0,1:T(8,128)(2,1)}, u32[]{:S(2)}, u32[]{:S(2)}) collective-permute-start(bf16[64,1024]{0,1:T(8,128)(2,1)S(1)} %fusion.56), channel_id=1, source_target_pairs={{0,16},{4,20},{8,24},{12,28},{16,0},{20,4},{24,8},{28,12},{1,17},{... | collective-permute-start | bytes 393224 | tf_op jit(solution)/shard_map/ppermute | solution.py:60
  259.2 51.0 %all-to-all-start.3 = ((bf16[4,256,1024]{2,1,0:T(8,128)(2,1)}), bf16[4,256,1024]{2,1,0:T(8,128)(2,1)S(1)}, u32[]{:S(2)}, u32[]{:S(2)}) async-start(bf16[4,256,1024]{2,1,0:T(8,128)(2,1)} %bitcast.277), calls=%async_computation.3 | async-start | bytes 4194304 | tf_op jit(solution)/shard_map/all_to_all | solution.py:56
  310.1 29.6 %all-to-all-start.4 = ((bf16[4,1024,128]{2,1,0:T(8,128)(2,1)}), bf16[4,1024,128]{2,1,0:T(8,128)(2,1)}, u32[]{:S(2)}, u32[]{:S(2)}) async-start(bf16[4,1024,128]{2,1,0:T(8,128)(2,1)} %pad_maximum_fusion.1), calls=%async_computation.4 | async-start | bytes 2097152 | tf_op jit(solution)/shard_map/all_to_all | solution.py:56
  386.9 31.8 %collective-permute-start.51 = (f32[10,256,256]{2,1,0:T(8,128)}, f32[10,256,256]{2,1,0:T(8,128)}, u32[]{:S(2)}, u32[]{:S(2)}) collective-permute-start(f32[10,256,256]{2,1,0:T(8,128)} %gram.1.ga_ref), channel_id=1, source_target_pairs={{0,4},{4,0},{8,12},{12,8},{16,20},{20,16},{24,28},{28,24},{1,5},{5... | collective-permute-start | bytes 7864328 | tf_op jit(solution)/shard_map/ppermute | solution.py:60
  412.7 55.3 %all-to-all-start.6 = ((bf16[4,256,1024]{2,1,0:T(8,128)(2,1)}), bf16[4,256,1024]{2,1,0:T(8,128)(2,1)S(1)}, u32[]{:S(2)}, u32[]{:S(2)}) async-start(bf16[4,256,1024]{2,1,0:T(8,128)(2,1)} %bitcast.278), calls=%async_computation.6 | async-start | bytes 4194304 | tf_op jit(solution)/shard_map/all_to_all | solution.py:56
  467.9 47.7 %all-to-all-start.7 = ((bf16[4,256,512]{2,1,0:T(8,128)(2,1)}), bf16[4,256,512]{2,1,0:T(8,128)(2,1)}, u32[]{:S(2)}, u32[]{:S(2)}) async-start(bf16[4,256,512]{2,1,0:T(8,128)(2,1)} %orthogonalize.1), calls=%async_computation.7 | async-start | bytes 2097152 | tf_op jit(solution)/shard_map/all_to_all | solution.py:56
  476.2 34.5 %collective-permute-start.47 = (bf16[3,256,512]{2,1,0:T(8,128)(2,1)S(1)}, bf16[3,256,512]{2,1,0:T(8,128)(2,1)}, u32[]{:S(2)}, u32[]{:S(2)}) collective-permute-start(bf16[3,256,512]{2,1,0:T(8,128)(2,1)S(1)} %pad_maximum_fusion.3.refs_0_), channel_id=1, source_target_pairs={{0,16},{4,20},{8,24},{12,28},{16,0},{20,4},{24,8},{28,12},{1,17},{... | collective-permute-start | bytes 2359304 | tf_op jit(solution)/shard_map/ppermute | solution.py:60
  477.0 33.8 %collective-permute-start.45 = (bf16[3,256,512]{2,1,0:T(8,128)(2,1)S(1)}, bf16[3,256,512]{2,1,0:T(8,128)(2,1)}, u32[]{:S(2)}, u32[]{:S(2)}) collective-permute-start(bf16[3,256,512]{2,1,0:T(8,128)(2,1)S(1)} %pad_maximum_fusion.3.refs_0_), channel_id=1, source_target_pairs={{0,8},{4,12},{8,0},{12,4},{16,24},{20,28},{24,16},{28,20},{1,9},{5... | collective-permute-start | bytes 2359304 | tf_op jit(solution)/shard_map/ppermute | solution.py:60
  478.4 46.7 %collective-permute-start.44 = (bf16[3,256,512]{2,1,0:T(8,128)(2,1)S(1)}, bf16[3,256,512]{2,1,0:T(8,128)(2,1)}, u32[]{:S(2)}, u32[]{:S(2)}) collective-permute-start(bf16[3,256,512]{2,1,0:T(8,128)(2,1)S(1)} %pad_maximum_fusion.3.refs_0_), channel_id=1, source_target_pairs={{0,4},{4,0},{8,12},{12,8},{16,20},{20,16},{24,28},{28,24},{1,5},{5... | collective-permute-start | bytes 2359304 | tf_op jit(solution)/shard_map/ppermute | solution.py:60
  495.8 31.6 %collective-permute-start.50 = (bf16[3,256,512]{2,1,0:T(8,128)(2,1)}, bf16[3,256,512]{2,1,0:T(8,128)(2,1)}, u32[]{:S(2)}, u32[]{:S(2)}) collective-permute-start(bf16[3,256,512]{2,1,0:T(8,128)(2,1)} %collective-permute-done.49.refs_6_), channel_id=1, source_target_pairs={{0,4},{4,0},{8,12},{12,8},{16,20},{20,16},{24,28},{28,24},{1,5},{5... | collective-permute-start | bytes 2359304 | tf_op jit(solution)/shard_map/ppermute | solution.py:60
  523.6 30.2 %collective-permute-start.58 = (bf16[3,256,512]{2,1,0:T(8,128)(2,1)}, bf16[3,256,512]{2,1,0:T(8,128)(2,1)}, u32[]{:S(2)}, u32[]{:S(2)}) collective-permute-start(bf16[3,256,512]{2,1,0:T(8,128)(2,1)} %pad_maximum_fusion.4.refs_0_), channel_id=1, source_target_pairs={{0,16},{4,20},{8,24},{12,28},{16,0},{20,4},{24,8},{28,12},{1,17},{... | collective-permute-start | bytes 2359304 | tf_op jit(solution)/shard_map/ppermute | solution.py:60
  525.0 30.7 %collective-permute-start.56 = (bf16[3,256,512]{2,1,0:T(8,128)(2,1)}, bf16[3,256,512]{2,1,0:T(8,128)(2,1)}, u32[]{:S(2)}, u32[]{:S(2)}) collective-permute-start(bf16[3,256,512]{2,1,0:T(8,128)(2,1)} %pad_maximum_fusion.4.refs_0_), channel_id=1, source_target_pairs={{0,8},{4,12},{8,0},{12,4},{16,24},{20,28},{24,16},{28,20},{1,9},{5... | collective-permute-start | bytes 2359304 | tf_op jit(solution)/shard_map/ppermute | solution.py:60
  (105 other events, 1513.3 us)
where the time goes:
time: 590 us; the launch traced here: 584 us
  waiting for transfers between devices  180 us (31%)
  Pallas kernels  156 us (26%)
  starting transfers between devices  112 us (19%)
  local copies, waits for them, and re-layouts  51.4 us (9%)
  other arithmetic  45.6 us (8%)
  matrix products  36.4 us (6%)
    ppermute x52, waiting for transfers between devices, xor_swap(): return lax.ppermute(x, 'rep', [(i, i ^ mask) for i in range(nr)])  104 us
    all_to_all x9, starting transfers between devices, z_exchange(): return lax.all_to_all(x, 'fsdp', split_axis=0, concat_axis=0, tiled=True)  49.3 us
    pallas_call x1, Pallas kernels, orthogonalize(): pl.pallas_call(ortho_kernel, in_specs=[pl.BlockSpec(memory_space=pltpu.SM...  49.2 us
    all_to_all x9, waiting for transfers between devices, z_exchange(): return lax.all_to_all(x, 'fsdp', split_axis=0, concat_axis=0, tiled=True)  43.5 us
    ppermute x52, starting transfers between devices, xor_swap(): return lax.ppermute(x, 'rep', [(i, i ^ mask) for i in range(nr)])  38.8 us
    pallas_call x2, Pallas kernels, finish(): pl.pallas_call(kernel, grid=(steps,), in_specs=[pl.BlockSpec(memory_space...  33.5 us
    ppermute x4, waiting for transfers between devices, z_gather(): lax.ppermute(left, 'fsdp', [(i, i - step) for i in range(step, nf - 1)])  32.5 us
    pallas_call x1, Pallas kernels, attend_back(): pl.pallas_call(attend_back_kernel, grid=(pairs,), in_specs=[mine, mine, m...  17.5 us
  transfers between devices with their start and end apart: 73, of which 24 were waited for; matrix products, arithmetic and copies ran while one was open for 22% of the time, Pallas kernels for 23%

commit v1 on v0

--- a/solution.py
+++ b/solution.py
@@ -103,21 +103,6 @@
 
 def listed(pieces):
     return [(d, n, len(pieces[d]), part) for d in sorted(pieces) for n, part in enumerate(pieces[d])]
-
-
-def halve(x, axis, bit, nr):
-    mine = lax.dynamic_index_in_dim(x, rep_bit(bit), axis, keepdims=False)
-    other = lax.dynamic_index_in_dim(x, 1 - rep_bit(bit), axis, keepdims=False)
-    return mine + xor_swap(other.astype(BF), 1 << bit, nr).astype(F32)
-
-
-def plane_sum(x, order, nr):
-    held = high_bits(nr)
-    x = x.reshape((2,) * len(held) + x.shape[1:])
-    for bit in order:
-        x = halve(x, sum(1 for b in held if b > bit), bit, nr)
-        held.remove(bit)
-    return x
 
 
 def plane_sum_small(x, nr):
@@ -161,7 +146,7 @@
             last = jnp.where(row >= col, s[:, i * QB :], -1e30)
             s = last if i == 0 else jnp.concatenate([s[:, : i * QB], last], axis=1)
             e = jnp.exp(s - jnp.max(s, axis=1, keepdims=True))
-            p = (e / jnp.sum(e, axis=1, keepdims=True)).astype(BF)
+            p = (e * (1.0 / jnp.sum(e, axis=1, keepdims=True))).astype(BF)
             p_ref[h, rows, :seen] = p
             o_ref[rows, lanes] = contract(p, v_ref[:seen, lanes], 1, 0).astype(BF)
 
@@ -187,49 +172,100 @@
     )(projected, projected, projected, *tables)
 
 
-def attend_back_kernel(q_ref, k_ref, v_ref, p_ref, do_ref, c_ref, lo_ref, hi_ref, dq_ref, dk_ref, dv_ref, ds_ref, acc_ref):
-    length = q_ref.shape[0]
+def attend_back(core, q, k, v, probs, cot, out_weight, mixed, normed, tables, unit):
+    length, width = q.shape
+    lanes = 2 * HEAD_DIM
+    pairs = width // lanes
+    model = cot.shape[1]
     blocks = length // QB
-    for h in range(2):
-        lanes = slice(h * HEAD_DIM, (h + 1) * HEAD_DIM)
-        for i in range(blocks):
-            rows = slice(i * QB, (i + 1) * QB)
-            seen = (i + 1) * QB
-            p = p_ref[h, rows, :seen].astype(F32)
-            row = lax.broadcasted_iota(jnp.int32, (QB, seen), 0) + i * QB
-            col = lax.broadcasted_iota(jnp.int32, (QB, seen), 1)
-            p = jnp.where(row >= col, p, 0.0)
-            dp = contract(do_ref[rows, lanes], v_ref[:seen, lanes], 1, 1)
-            ds = (p * (dp - jnp.sum(p * dp, axis=1, keepdims=True))).astype(BF)
-            ds_ref[rows, :seen] = ds
-            acc_ref[0, rows, lanes] = contract(ds, k_ref[:seen, lanes], 1, 0) * HEAD_DIM ** (-0.5)
-        for j in range(blocks):
-            cols = slice(j * QB, (j + 1) * QB)
-            rest = slice(j * QB, length)
-            acc_ref[1, cols, lanes] = contract(ds_ref[rest, cols], q_ref[rest, lanes], 0, 0)
-            acc_ref[2, cols, lanes] = contract(p_ref[h, rest, cols], do_ref[rest, lanes], 0, 0)
-    cosine, low, high = c_ref[...], -lo_ref[...], -hi_ref[...]
-    dq_ref[...] = turn(acc_ref[0], cosine, low, high).astype(BF)
-    dk_ref[...] = turn(acc_ref[1], cosine, low, high).astype(BF)
-    dv_ref[...] = acc_ref[2].astype(BF)
-
-
-def attend_back(q, k, v, probs, d_mixed, tables):
-    length, width = q.shape
-    pairs = width // (2 * HEAD_DIM)
-    block = (length, 2 * HEAD_DIM)
-    whole = pl.BlockSpec(block, lambda h: (0, 0))
-    mine = pl.BlockSpec(block, lambda h: (0, h))
-    piece = jax.ShapeDtypeStruct((length, width), BF)
-    return pl.pallas_call(
-        attend_back_kernel,
-        grid=(pairs,),
-        in_specs=[mine, mine, mine, pl.BlockSpec((2, length, length), lambda h: (h, 0, 0)), mine, whole, whole, whole],
-        out_specs=[mine, mine, mine],
-        out_shape=[piece, piece, piece],
-        scratch_shapes=[pltpu.VMEM((length, length), BF), pltpu.VMEM((3,) + block, F32)],
+    group = lanes // unit
+    half_rot = ROT // 2
+
+    def kernel(
+        w_ref, q_ref, k_ref, v_ref, p_ref, y_ref, o_ref, m_ref, x_ref, c_ref, lo_ref, hi_ref,
+        d_ref, other_ref, own_ref, do_ref, turned, ds_ref, acc
+    ):
+        do = contract(y_ref[...], o_ref[...], 1, 1).astype(BF)
+        do_ref[...] = do
+        for n, x in enumerate((q_ref[...], k_ref[...], do)):
+            turned[n] = x.T
+        for h in range(2):
+            at = slice(h * HEAD_DIM, (h + 1) * HEAD_DIM)
+            for i in range(blocks):
+                rows = slice(i * QB, (i + 1) * QB)
+                seen = (i + 1) * QB
+                p = p_ref[h, rows, :seen].astype(F32)
+                dp = contract(do_ref[rows, at], v_ref[:seen, at], 1, 1)
+                ds = (p * (dp - jnp.sum(p * dp, axis=1, keepdims=True))).astype(BF)
+                ds_ref[rows, :seen] = ds
+                acc[0, at, rows] = contract(turned[1, at, :seen], ds, 1, 1) * HEAD_DIM ** (-0.5)
+            for j in range(blocks):
+                cols = slice(j * QB, (j + 1) * QB)
+                rest = slice(j * QB, length)
+                acc[1, at, cols] = contract(turned[0, at, rest], ds_ref[rest, cols], 1, 0)
+                acc[2, at, cols] = contract(turned[2, at, rest], p_ref[h, rest, cols], 1, 0)
+        cosine, low, high = c_ref[...], lo_ref[...], hi_ref[...]
+        for n in range(2):
+            x = acc[n]
+            x = x * cosine - pltpu.roll(x, half_rot, 0) * low - pltpu.roll(x, lanes - half_rot, 0) * high
+            d_ref[n] = x.astype(BF)
+        d_ref[2] = acc[2].astype(BF)
+        for n in range(4):
+            left = m_ref[...].T if n == 3 else d_ref[n]
+            grad = contract(left, y_ref[...] if n == 3 else x_ref[...], 1, 0).reshape(group, unit, model)
+
+            @pl.when(w_ref[0] == n // 2)
+            def _(n=n, grad=grad):
+                own_ref[n % 2, 0] = grad
+
+            @pl.when(w_ref[0] != n // 2)
+            def _(n=n, grad=grad):
+                other_ref[n % 2, 0] = grad.astype(BF)
+
+    block = (length, lanes)
+    mine = pl.BlockSpec(block, lambda h, w: (0, h))
+    table = pl.BlockSpec(block[::-1], lambda h, w: (0, 0))
+    whole = pl.BlockSpec((length, model), lambda h, w: (0, 0))
+    grads = pl.BlockSpec((2, 1, group, unit, model), lambda h, w: (0, h, 0, 0, 0))
+    shape = (2, pairs, group, unit, model)
+    d_all, other, own = pl.pallas_call(
+        kernel,
+        grid_spec=pltpu.PrefetchScalarGridSpec(
+            num_scalar_prefetch=1,
+            grid=(pairs,),
+            in_specs=[
+                mine,
+                mine,
+                mine,
+                pl.BlockSpec((2, length, length), lambda h, w: (h, 0, 0)),
+                whole,
+                pl.BlockSpec((lanes, model), lambda h, w: (h, 0)),
+                mine,
+                whole,
+                table,
+                table,
+                table,
+            ],
+            out_specs=[pl.BlockSpec((3, lanes, length), lambda h, w: (0, h, 0)), grads, grads],
+            scratch_shapes=[
+                pltpu.VMEM(block, BF),
+                pltpu.VMEM((3,) + block[::-1], BF),
+                pltpu.VMEM((length, length), BF),
+                pltpu.VMEM((3,) + block[::-1], F32),
+            ],
+        ),
+        out_shape=[
+            jax.ShapeDtypeStruct((3, width, length), BF),
+            jax.ShapeDtypeStruct(shape, BF),
+            jax.ShapeDtypeStruct(shape, F32),
+        ],
+        cost_estimate=pl.CostEstimate(
+            flops=24 * length * length * width, transcendentals=0, bytes_accessed=8 * length * length
+        ),
         name="attend_back",
-    )(q, k, v, probs, d_mixed, *tables)
+    )(core.astype(jnp.int32).reshape(1), q, k, v, probs, cot, out_weight, mixed, normed, *[t.T for t in tables])
+    flat = (2 * pairs * group, unit, model)
+    return d_all.reshape(3 * width, length), other.reshape(flat), own.reshape(flat)
 
 
 def split(x):
@@ -369,24 +405,43 @@
     )(swapped.astype(jnp.int32).reshape(1), gram_a, gram_b, cols)
 
 
-def momentum_cols(active, moment, grads):
+def momentum_cols(mode, moment, grads):
     nf, size, unit = grads.shape
-
-    def kernel(flag_ref, m_ref, g_ref, out_ref):
-        keep = jnp.full((size, unit), flag_ref[0], jnp.int32) == 1
-        for b in range(nf):
-            lanes = slice(b * unit, (b + 1) * unit)
-            total = m_ref[:, lanes].astype(F32) + g_ref[b].astype(F32)
-            out_ref[:, lanes] = jnp.where(keep, total, 0.0).astype(BF)
+    rows = size // nf
+
+    def kernel(mode_ref, m_ref, g_ref, out_ref):
+        def fill(pick):
+            for a in range(nf):
+                for b in range(nf):
+                    at = (slice(a * rows, (a + 1) * rows), slice(b * unit, (b + 1) * unit))
+                    out_ref[at] = pick(a, b)
+
+        def block(a, b):
+            return m_ref[a, :, b * unit : (b + 1) * unit].astype(F32)
+
+        def grad(a, b):
+            return g_ref[b, a * rows : (a + 1) * rows].astype(F32)
+
+        @pl.when(mode_ref[0] == 0)
+        def _():
+            out_ref[...] = jnp.zeros(out_ref.shape, BF)
+
+        @pl.when(mode_ref[0] == 1)
+        def _():
+            fill(lambda a, b: (block(a, b) + grad(a, b)).astype(BF))
+
+        @pl.when(mode_ref[0] == 2)
+        def _():
+            fill(lambda a, b: (block(b, a) + grad(a, b)).astype(BF))
 
     vmem = pl.BlockSpec(memory_space=pltpu.VMEM)
     return pl.pallas_call(
         kernel,
         in_specs=[pl.BlockSpec(memory_space=pltpu.SMEM), vmem, vmem],
         out_specs=vmem,
-        out_shape=jax.ShapeDtypeStruct(moment.shape, BF),
+        out_shape=jax.ShapeDtypeStruct((size, nf * unit), BF),
         name="momentum_cols",
-    )(active.astype(jnp.int32).reshape(1), moment, grads)
+    )(mode.astype(jnp.int32).reshape(1), moment, grads)
 
 
 def rep_scalar():
@@ -418,79 +473,185 @@
     )(rep_scalar(), *[part for _, _, _, part in entries])
 
 
-def grad_mlp(which, d_pre, normed, hidden, cot, blocks, dtype):
+def feed_forward(core, normed, cot, slab, bias, lanes):
     length, width = normed.shape
-    mid = d_pre.shape[1] // 2
+    total = slab.shape[1] // 2
+    mid = total // 2
     step = min(mid, QB)
     count = mid // step
-    unit = mid // blocks
-
-    def kernel(w_ref, a_ref, x_ref, b_ref, y_ref, out_ref):
-        def put(left, right):
-            out_ref[0] = contract(left[...], right[...], 0, 0).reshape(step // unit, unit, width).astype(dtype)
-
-        @pl.when(pl.program_id(0) == 0)
+    unit = mid // lanes
+    group = step // unit
+    root = (2.0 / 3.141592653589793) ** 0.5
+
+    def kernel(w_ref, x_ref, y_ref, up_ref, down_ref, b_ref, h_ref, d_ref, sum_ref, other_ref, gu_ref, gd_ref):
+        x, y = x_ref[...], y_ref[...]
+        v = contract(x, up_ref[...], 1, 0) + b_ref[...]
+        t = jnp.tanh(root * (v + 0.044715 * (v * v * v)))
+        hidden = (0.5 * v * (1.0 + t)).astype(BF)
+        slope = 0.5 * (1.0 + t) + 0.5 * v * (1.0 - t * t) * (root * (1.0 + 3 * 0.044715 * (v * v)))
+        d_pre = (contract(y, down_ref[...], 1, 0) * slope).astype(BF)
+        h_ref[...] = hidden
+        d_ref[...] = d_pre
+        sum_ref[...] = jnp.sum(d_pre.astype(F32), axis=0, keepdims=True)
+        up = contract(d_pre, x, 0, 0).reshape(group, unit, width)
+        down = contract(hidden, y, 0, 0).reshape(group, unit, width)
+
+        @pl.when(pl.program_id(0) < count)
         def _():
-            put(a_ref, x_ref)
-
-        @pl.when(pl.program_id(0) == 1)
+            other_ref[0] = up.astype(BF)
+            other_ref[1] = down.astype(BF)
+
+        @pl.when(pl.program_id(0) >= count)
         def _():
-            put(b_ref, y_ref)
-
-    whole = pl.BlockSpec((length, width), lambda m, i, w: (0, 0))
+            gu_ref[...] = up
+            gd_ref[...] = down
+
+    def at(i, w):
+        return jnp.where(i < count, (1 - w[0]) * count + i, w[0] * count + i - count)
+
+    whole = pl.BlockSpec((length, width), lambda i, w: (0, 0))
+    tall = pl.BlockSpec((length, step), lambda i, w: (0, at(i, w)))
+    own = pl.BlockSpec((group, unit, width), lambda i, w: (jnp.maximum(i - count, 0), 0, 0))
     return pl.pallas_call(
         kernel,
         grid_spec=pltpu.PrefetchScalarGridSpec(
             num_scalar_prefetch=1,
-            grid=(2, count),
+            grid=(2 * count,),
             in_specs=[
-                pl.BlockSpec((length, step), lambda m, i, w: (0, w[0] * count + jnp.where(m == 0, i, count - 1))),
                 whole,
-                pl.BlockSpec((length, step), lambda m, i, w: (0, w[0] * count + jnp.where(m == 1, i, 0))),
                 whole,
+                pl.BlockSpec((width, step), lambda i, w: (0, at(i, w))),
+                pl.BlockSpec((width, step), lambda i, w: (0, 2 * count + at(i, w))),
+                pl.BlockSpec((1, step), lambda i, w: (0, at(i, w))),
             ],
-            out_specs=pl.BlockSpec((1, step // unit, unit, width), lambda m, i, w: (m, i, 0, 0)),
+            out_specs=[
+                tall,
+                tall,
+                pl.BlockSpec((1, step), lambda i, w: (0, at(i, w))),
+                pl.BlockSpec((2, group, unit, width), lambda i, w: (0, jnp.minimum(i, count - 1), 0, 0)),
+                own,
+                own,
+            ],
         ),
-        out_shape=jax.ShapeDtypeStruct((2, blocks, unit, width), dtype),
+        out_shape=[
+            jax.ShapeDtypeStruct((length, total), BF),
+            jax.ShapeDtypeStruct((length, total), BF),
+            jax.ShapeDtypeStruct((1, total), F32),
+            jax.ShapeDtypeStruct((2, lanes, unit, width), BF),
+            jax.ShapeDtypeStruct((lanes, unit, width), F32),
+            jax.ShapeDtypeStruct((lanes, unit, width), F32),
+        ],
         cost_estimate=pl.CostEstimate(
-            flops=4 * length * mid * width, transcendentals=0, bytes_accessed=8 * length * width
+            flops=8 * length * width * total, transcendentals=length * total, bytes_accessed=20 * length * width
         ),
-        name="grad_mlp",
-    )(which.astype(jnp.int32).reshape(1), d_pre, normed, hidden, cot)
-
-
-def grad_comb(which, dq, dk, dv, mixed, normed, cot, blocks, dtype):
-    length, width = normed.shape
-    step = dq.shape[1]
-    unit = 2 * step // blocks
-
-    def kernel(w_ref, q_ref, k_ref, v_ref, m_ref, x_ref, y_ref, out_ref):
-        def put(left, right):
-            out_ref[...] = contract(left[...], right[...], 0, 0).reshape(step // unit, unit, width).astype(dtype)
-
-        at = 2 * w_ref[0] + pl.program_id(0)
-        for n, (left, right) in enumerate(((q_ref, x_ref), (k_ref, x_ref), (v_ref, x_ref), (m_ref, y_ref))):
-
-            @pl.when(at == n)
-            def _(left=left, right=right):
-                put(left, right)
-
-    left = pl.BlockSpec((length, step), lambda i, w: (0, 0))
-    whole = pl.BlockSpec((length, width), lambda i, w: (0, 0))
+        name="feed_forward",
+    )(core.astype(jnp.int32).reshape(1), normed, cot, slab, slab, bias)
+
+
+def fold(items):
+    shapes, arrays = [], []
+    for own, (got, _), cut, _, _ in items:
+        rows = cut.stop - cut.start
+        shapes += [
+            jax.ShapeDtypeStruct((own.shape[0] // 2, rows, own.shape[2]), BF),
+            jax.ShapeDtypeStruct((own.shape[0] // 2, rows, own.shape[2]), F32),
+        ]
+        arrays += [own, got]
+    count = len(items)
+
+    def kernel(r_ref, *refs):
+        ins, outs = refs[: 2 * count], refs[2 * count :]
+        for k, (own, (_, index), cut, held, bit) in enumerate(items):
+            low = sum(1 for b in held if b < bit)
+            value = (r_ref[0] >> bit) & 1
+            for n in range(own.shape[0] // 2):
+                base = ((n >> low) << (low + 1)) | (n & ((1 << low) - 1))
+
+                def total(choice, k=k, base=base, low=low, cut=cut, index=index):
+                    at = base | (choice << low)
+                    got = ins[2 * k + 1][at, cut] if index is None else ins[2 * k + 1][index, at, cut]
+                    return ins[2 * k][at, cut] + got.astype(F32)
+
+                outs[2 * k][n] = total(1 - value).astype(BF)
+                outs[2 * k + 1][n] = total(value)
+
+    vmem = pl.BlockSpec(memory_space=pltpu.VMEM)
+    flat = pl.pallas_call(
+        kernel,
+        in_specs=[pl.BlockSpec(memory_space=pltpu.SMEM)] + [vmem] * (2 * count),
+        out_specs=[vmem] * (2 * count),
+        out_shape=shapes,
+    )(rep_scalar(), *arrays)
+    return [(flat[2 * k], flat[2 * k + 1]) for k in range(count)]
+
+
+def units_kernel(parts, nf):
+    flat = [x for part in parts for pair in part for x in pair]
+    unit = sum(x.shape[0] for x, _ in parts[0])
+    width = flat[0].shape[1]
+    rows = width // nf
+
+    def kernel(*refs):
+        ins, plane_ref, row_ref = refs[:-2], refs[-2], refs[-1]
+        n = 0
+        for m, part in enumerate(parts):
+            blocks = []
+            for _ in part:
+                blocks.append(ins[n][...] + ins[n + 1][...].astype(F32))
+                n += 2
+            block = (blocks[0] if len(blocks) == 1 else jnp.concatenate(blocks, axis=0)).T.astype(BF)
+            for to in ((0, 1), (2,), (3,))[m]:
+                plane_ref[to] = block
+            for b in range(nf):
+                row_ref[b, m] = block[b * rows : (b + 1) * rows]
+        for to in range(4, nf):
+            plane_ref[to] = jnp.zeros((width, unit), BF)
+
+    vmem = pl.BlockSpec(memory_space=pltpu.VMEM)
+    return pl.pallas_call(
+        kernel,
+        in_specs=[vmem] * len(flat),
+        out_specs=[vmem] * 2,
+        out_shape=[
+            jax.ShapeDtypeStruct((nf, width, unit), BF),
+            jax.ShapeDtypeStruct((nf, 3, rows, unit), BF),
+        ],
+        name="units",
+    )(*flat)
+
+
+def moment_units(spot, qkv, out, up, down, nf, nr):
+    rows, width = out.shape
+    unit = up.shape[1] // (nf * nr)
+    per = nr // 4
+    units = 3 * per
+
+    def kernel(s_ref, q_ref, o_ref, u_ref, d_ref, out_ref):
+        for n, block in enumerate((q_ref[...], o_ref[...].T, u_ref[...], d_ref[...])):
+            out_ref[n] = (MOMENTUM_RATE * block).astype(BF)
+        for n in range(4, nf):
+            out_ref[n] = jnp.zeros((rows, unit), BF)
+
+    def qkv_at(b, s):
+        inside = jnp.minimum(s[0], units - 1)
+        return (0, (inside // per) * (width // unit) + b * per + inside % per)
+
     return pl.pallas_call(
         kernel,
         grid_spec=pltpu.PrefetchScalarGridSpec(
             num_scalar_prefetch=1,
-            grid=(2,),
-            in_specs=[left] * 4 + [whole] * 2,
-            out_specs=pl.BlockSpec((step // unit, unit, width), lambda i, w: (i, 0, 0)),
+            grid=(nf,),
+            in_specs=[
+                pl.BlockSpec((rows, unit), qkv_at),
+                pl.BlockSpec((unit, rows), lambda b, s: (jnp.maximum(s[0] - units, 0), b)),
+                pl.BlockSpec((rows, unit), lambda b, s: (0, b * nr + s[0])),
+                pl.BlockSpec((rows, unit), lambda b, s: (0, b * nr + s[0])),
+            ],
+            out_specs=pl.BlockSpec((nf, rows, unit), lambda b, s: (0, 0, b)),
         ),
-        out_shape=jax.ShapeDtypeStruct((blocks, unit, width), dtype),
-        cost_estimate=pl.CostEstimate(
-            flops=4 * length * step * width, transcendentals=0, bytes_accessed=8 * length * width
-        ),
-        name="grad_comb",
-    )(which.astype(jnp.int32).reshape(1), dq, dk, dv, mixed, normed, cot)
+        out_shape=jax.ShapeDtypeStruct((nf, rows, nf * unit), BF),
+        name="moment_units",
+    )(spot.astype(jnp.int32).reshape(1), qkv, out, up, down)
 
 
 def grad_rule(block, have):
@@ -504,7 +665,7 @@
     return rule
 
 
-def finish_plain(pieces, have, rules, nr):
+def finish_plain(pieces, have, rules, nr, subset):
     whole = jnp.stack([jnp.concatenate(pieces[d], axis=1) for d in sorted(pieces)])
     index = jnp.arange(nr)
     source = (index // (nr // 2)) | ((index % (nr // 2)) << 1)
@@ -518,10 +679,11 @@
     out = whole[3 * per :, 0].transpose(0, 3, 2, 1).reshape(rows, -1)
     up = whole[:, 1].transpose(1, 2, 0, 3).reshape(rows, -1)
     down = whole[:, 2].transpose(1, 2, 0, 3).reshape(rows, -1)
-    return [rule(m.astype(F32), x) for m, x, rule in zip((qkv, out, up, down), have, rules)]
-
-
-def finish(pieces, have, rules, outs, nr):
+    whole = (qkv, out, up, down)
+    return [rules[m](whole[m].astype(F32), have[m]) for m in subset]
+
+
+def finish(pieces, have, rules, outs, nr, subset):
     entries = listed(pieces)
     parts = [part for _, _, _, part in entries]
     wide = parts[0].shape[2]
@@ -529,16 +691,18 @@
     nf = have[1].shape[1] // rows
     u = wide // nf
     if u % 128:
-        return finish_plain(pieces, have, rules, nr)
+        return finish_plain(pieces, have, rules, nr, subset)
     per = nr // 4
-    order = [(2, 1, nf), (3, 2, nf), (0, 0, 3), (1, 0, 1)]
-    starts = [0, nf, 2 * nf, 2 * nf + 3]
-    steps = 2 * nf + 4
+    order = [x for x in ((2, 1, nf), (3, 2, nf), (0, 0, 3), (1, 0, 1)) if x[0] in subset]
+    starts = [sum(x[2] for x in order[:n]) for n in range(len(order))]
+    steps = sum(x[2] for x in order)
+    spot = {matrix: n for n, matrix in enumerate(subset)}
+    many = len(subset)
 
     def kernel(r_ref, *refs):
         ins = refs[: len(parts)]
-        have_refs = refs[len(parts) : len(parts) + 4]
-        out_refs = refs[len(parts) + 4 : len(parts) + 4 + 4 * outs]
+        have_refs = refs[len(parts) : len(parts) + many]
+        out_refs = refs[len(parts) + many : len(parts) + many + many * outs]
         slab, sems = refs[-2:]
         step = pl.program_id(0)
 
@@ -549,14 +713,14 @@
 
         @pl.when(step == 0)
         def _():
-            for which in (1, 2, 0):
+            for which in dict.fromkeys(x[1] for x in order):
                 for copy in copies(which):
                     copy.start()
 
         def write(matrix, at, block):
-            values = rules[matrix](block.astype(F32), have_refs[matrix][at])
+            values = rules[matrix](block.astype(F32), have_refs[spot[matrix]][at])
             for n, value in enumerate(values):
-                out_refs[matrix * outs + n][at] = value
+                out_refs[spot[matrix] * outs + n][at] = value
 
         for (matrix, which, count), start in zip(order, starts):
             for k in range(count):
@@ -581,13 +745,14 @@
                                 at = (slice(s * u, (s + 1) * u), slice(b * rows, (b + 1) * rows))
                                 write(1, at, slab[3 * per + s, 0, :, b * u : (b + 1) * u].astype(F32).T)
 
-    specs = [None] * 4
+    specs = [None] * many
     for (matrix, _, count), start in zip(order, starts):
-        specs[matrix] = pl.BlockSpec(
+        specs[spot[matrix]] = pl.BlockSpec(
             (rows, have[matrix].shape[1] // count),
             lambda i, start=start, count=count: (0, jnp.clip(i - start, 0, count - 1)),
         )
-    shapes = [jax.ShapeDtypeStruct(m.shape, F32) for m in have for _ in range(outs)]
+    taken = [have[m] for m in subset]
+    shapes = [jax.ShapeDtypeStruct(m.shape, F32) for m in taken for _ in range(outs)]
     flat = pl.pallas_call(
         kernel,
         grid=(steps,),
@@ -599,10 +764,10 @@
             pltpu.SemaphoreType.DMA((len(parts), 3)),
         ],
         cost_estimate=pl.CostEstimate(
-            flops=rows * rows * 100, transcendentals=0, bytes_accessed=(6 + 4 * outs) * sum(m.size for m in have)
+            flops=rows * rows * 100, transcendentals=0, bytes_accessed=(6 + 4 * outs) * sum(m.size for m in taken)
         ),
-    )(rep_scalar(), *parts, *have)
-    return [tuple(flat[m * outs : (m + 1) * outs]) for m in range(4)]
+    )(rep_scalar(), *parts, *taken)
+    return [tuple(flat[m * outs : (m + 1) * outs]) for m in range(many)]
 
 
 def layer_norm_parts(values):
@@ -610,10 +775,6 @@
     spread = jnp.mean(center * center, axis=-1, keepdims=True)
     scale = lax.rsqrt(spread + 1e-05)
     return center * scale, scale
-
-
-def gelu_tanh(values):
-    return jax.nn.gelu(values, approximate=True)
 
 
 def on_device(
@@ -678,85 +839,97 @@
 
     mlp = [jnp.concatenate(p, axis=1) for p in zip(by_dest(up_weight, 1), by_dest(down_weight, 1))]
     mlp = z_exchange(after(jnp.stack(mlp), got))
-    mlp = slab_of(mlp)
+    mlp_pieces = plane_pieces(mlp, 0, nr)
     tok_near = z_neighbours(tok, nf)
     cot_near = z_neighbours(after(cot, *tok_near), nf)
     tok_all = z_gather(tok, tok_near, nf)
     length = tok_all.shape[0]
-    cot_near = lax.optimization_barrier((*cot_near, tok_all))[:2]
-    cot_all = z_gather(cot, cot_near, nf)
-    up_cols, down_cols = mlp[:, :hidden_width], mlp[:, hidden_width:]
 
     xhat_all, _ = layer_norm_parts(tok_all.astype(F32))
     normed = (xhat_all * gain + beta).astype(BF)
     projected = jnp.dot(normed, qkv_cols, preferred_element_type=F32)
-    tables = rotary_tables(length)
-    q, k, v, probs, mixed = attend(projected, tables, head_width)
-    hidden_pre = jnp.dot(normed, up_cols, preferred_element_type=F32) + up_bias.astype(F32)
-    hidden_f, gelu_pull = jax.vjp(gelu_tanh, hidden_pre)
-    hidden = hidden_f.astype(BF)
+
+    def side_by_side(blocks):
+        return jnp.concatenate([blocks[b] for b in range(nf)], axis=1)
 
     def unit_columns(moment, thirds):
         step = moment.shape[1] // thirds
         wide = step // nf
         inside = jnp.minimum(spot, thirds * wide // unit - 1) * unit
         start = (inside // wide) * step + inside % wide
-        parts = [lax.dynamic_slice_in_dim(moment, start + b * wide, unit, 1) for b in range(nf)]
-        return jnp.concatenate(parts, axis=1)
-
-    def side_by_side(blocks):
-        return jnp.concatenate([blocks[b] for b in range(nf)], axis=1)
-
-    held = lax.optimization_barrier((qkv_moment, out_moment, up_moment, down_moment, normed))[:4]
-    out_start = jnp.maximum(spot - qkv_units, 0) * unit
-    out_rows = lax.dynamic_slice_in_dim(held[1], out_start, unit, 0).T
-    out_rows = side_by_side(out_rows.reshape(nf, rows, unit))
-    owned = [unit_columns(held[0], 3), out_rows, unit_columns(held[2], 1), unit_columns(held[3], 1)]
-    owned = [(MOMENTUM_RATE * m).astype(BF) for m in owned]
-    owned = owned + [jnp.zeros((rows, nf * unit), BF)] * (nf - 4)
-    moment_in = z_exchange(after(jnp.stack(owned), cot_all))
-    moment_out = [side_by_side(moment_in[:, :, b * unit : (b + 1) * unit]) for b in range(nf)]
-    moment_cols = jnp.where(out_plane, jnp.concatenate(moment_out, axis=0), moment_in.reshape(width, nf * unit))
-
-    d_hidden = jnp.dot(cot_all, down_cols, preferred_element_type=F32)
-    d_pre = gelu_pull(d_hidden)[0].astype(BF)
+        return jnp.concatenate([lax.dynamic_slice_in_dim(moment, start + b * wide, unit, 1) for b in range(nf)], axis=1)
+
+    held = lax.optimization_barrier((qkv_moment, out_moment, up_moment, down_moment, got))[:4]
+    if unit % 128:
+        out_start = jnp.maximum(spot - qkv_units, 0) * unit
+        out_rows = lax.dynamic_slice_in_dim(held[1], out_start, unit, 0).T
+        out_rows = side_by_side(out_rows.reshape(nf, rows, unit))
+        owned = [unit_columns(held[0], 3), out_rows, unit_columns(held[2], 1), unit_columns(held[3], 1)]
+        owned = [(MOMENTUM_RATE * m).astype(BF) for m in owned]
+        owned = jnp.stack(owned + [jnp.zeros((rows, nf * unit), BF)] * (nf - 4))
+    else:
+        owned = moment_units(spot, *held, nf, nr)
+    cot_near = lax.optimization_barrier((*cot_near, projected))[:2]
+    cot_all = z_gather(cot, cot_near, nf)
+    tables = rotary_tables(length)
+    q, k, v, probs, mixed = attend(projected, tables, head_width)
+    mlp_pieces = with_partner(mlp_pieces, nr)
+    mlp = assemble(mlp_pieces, nr).reshape(width, 2 * hidden_width)
+    up_cols, down_cols = mlp[:, :hidden_width], mlp[:, hidden_width:]
+    moment_in = z_exchange(after(owned, cot_all))
+
     lanes = nr // 2
-
-    def joined(mine, other):
-        return mine + xor_swap(other, 1, nr).astype(F32)
-
     order = high_bits(nr)
-    mlp_parts = (d_pre, normed, hidden, cot_all, lanes)
-    sum_mlp = joined(grad_mlp(core, *mlp_parts, F32), grad_mlp(1 - core, *mlp_parts, BF))
-    unit_up, unit_down = plane_sum(sum_mlp[0], order, nr), plane_sum(sum_mlp[1], order[::-1], nr)
-
-    d_mixed = contract(cot_all, out_weight, 1, 1).astype(BF)
-    dq, dk, dv = attend_back(q, k, v, probs, d_mixed, tables)
-    comb_parts = (dq, dk, dv, mixed, normed, cot_all, lanes)
-    sum_comb = joined(grad_comb(core, *comb_parts, F32), grad_comb(1 - core, *comb_parts, BF))
-    unit_comb = jnp.concatenate(
-        [
-            plane_sum(sum_comb[:, : unit // 2], order, nr),
-            plane_sum(sum_comb[:, unit // 2 :], order[::-1], nr),
-        ],
-        axis=0,
+    every = slice(0, unit)
+    hidden, d_pre, up_sum, other, grad_up, grad_down = feed_forward(
+        core, normed, cot_all, after(mlp, mixed), up_bias.astype(F32).reshape(1, hidden_width), lanes
     )
-
+    other = xor_swap(other, 1, nr)
+
+    def send(results, bits):
+        return [(own, (xor_swap(away, 1 << bit, nr), None)) for (away, own), bit in zip(results, bits)]
+
+    ways = (order, order[::-1])
+    state = [(grad_up, (other, 0)), (grad_down, (other, 1))]
+    steps = []
+    for n in range(len(order)):
+        bits = [way[n] for way in ways]
+        left = [[b for b in order if b not in way[:n]] for way in ways]
+        done = fold([(*x, every, h, b) for x, h, b in zip(state, left, bits)])
+        steps.append(done)
+        state = send(done, bits)
+        if n == 0:
+            q = after(q, *[x for pair in done for x in pair])
+            d_projected, other, grad_own = attend_back(
+                core, q, k, v, probs, cot_all, out_weight, mixed, normed, tables, unit
+            )
+    mlp_state = state
+    other = xor_swap(after(other, *[x for pair in steps[-1] for x in pair]), 1, nr)
+    state = [(grad_own, (other, None))] * 2
+    cuts = (slice(0, unit // 2), slice(unit // 2, unit))
+    for n in range(len(order)):
+        bits = [way[n] for way in ways]
+        left = [[b for b in order if b not in way[:n]] for way in ways]
+        if n:
+            cuts = (slice(0, unit // 2),) * 2
+        done = fold([(*x, c, h, b) for x, c, h, b in zip(state, cuts, left, bits)])
+        state = send(done, bits)
+    plane_send, grad_send = units_kernel(
+        [[(own[0], got[0]) for own, (got, _) in part] for part in (state, mlp_state[:1], mlp_state[1:])], nf
+    )
+
+    cut = 5 * local_len // 8
+    mixed, hidden = lax.optimization_barrier((mixed, hidden, grad_own))[:2]
     partial_out = jnp.dot(mixed, out_weight, preferred_element_type=F32) + contract(hidden, down_cols, 1, 1)
     partial_out = partial_out.astype(BF).reshape(nf, local_len, width)
-    summed = z_exchange(after(partial_out, moment_in))
-
-    units = [u.astype(BF).T for u in (unit_comb, unit_up, unit_down)]
-    sends = [units[0], units[0], units[1], units[2]] + [jnp.zeros((width, unit), BF)] * (nf - 4)
-    grad_cols = z_exchange(after(jnp.stack(sends), summed))
-    active = jnp.where(f == 0, ~is_out, jnp.where(f == 1, is_out, f < 4))
-    s_cols = momentum_cols(active, moment_cols, grad_cols)
+    summed = z_exchange(after(partial_out[:, :cut], moment_in))
+
+    grad_cols = z_exchange(after(plane_send, summed))
+    mode = jnp.where(f == 0, ~is_out, jnp.where(f == 1, 2 * is_out, f < 4))
+    s_cols = momentum_cols(mode, moment_in, grad_cols)
 
     s_pieces = plane_pieces(s_cols, 0, nr)
-    gram = gram_of(s_pieces)
-    gram_other = xor_swap(gram, 1, nr)
-
-    grad_send = jnp.stack([jnp.stack([u[b * rows : (b + 1) * rows] for b in range(nf)]) for u in units], axis=1)
+
     grad_got = z_exchange(after(grad_send, grad_cols))
     kept = jnp.where(is_out, grad_send[:, 0], grad_got[:, 0])
     grad_mine = [side_by_side(g) for g in (kept, grad_got[:, 1], grad_got[:, 2])]
@@ -765,37 +938,46 @@
     for mask in range(2, nr, 2):
         grad_pieces[mask] = (xor_swap(grad_mine, mask, nr),)
 
-    d_projected = jnp.concatenate([after(dq, grad_cols), dk, dv], axis=1)
-    partial_normed = contract(d_projected, qkv_cols, 1, 1) + contract(d_pre, up_cols, 1, 1)
+    d_projected = after(d_projected, grad_cols)
+    partial_normed = contract(d_projected, qkv_cols, 0, 1) + contract(d_pre, up_cols, 1, 1)
+    pair = jnp.stack([jnp.sum(partial_normed * xhat_all, axis=0), jnp.sum(partial_normed, axis=0)])
+    pair = pair.reshape(2, nf, rows).transpose(1, 0, 2)
+    pair = jnp.pad(pair, ((0, 0), (0, 6), (0, width - rows))).astype(BF)
     partial_normed = partial_normed.astype(BF).reshape(nf, local_len, width)
-    summed_normed = z_exchange(after(partial_normed, grad_got))
+    late = jnp.concatenate([partial_normed, partial_out[:, cut:], pair], axis=1)
+    gram = gram_of(lax.optimization_barrier((s_pieces, late))[0])
+    gram_other = xor_swap(gram, 1, nr)
+    late = z_exchange(after(late, grad_got))
 
     ortho = orthogonalize(out_plane, gram, gram_other, s_cols, nf)
-    back = z_exchange(after(ortho, summed_normed))
+    back = z_exchange(after(ortho, late))
+    late = after(late, back)
     ortho_mine = jnp.stack([jnp.where(is_out, back[1], back[0]), back[2], back[3]])
     ortho_pieces = with_partner(plane_pieces(ortho_mine, 1, nr), nr)
 
     mats = (qkv_weight, out_weight, up_weight, down_weight)
     moments = (qkv_moment, out_moment, up_moment, down_moment)
-    done = finish(with_partner(grad_pieces, nr), moments, [grad_rule] * 4, 2, nr)
+    grad_pieces = with_partner(grad_pieces, nr)
+    grad_rules = [grad_rule] * 4
+    done = finish(grad_pieces, moments, grad_rules, 2, nr, (0, 1, 2, 3))
     grads, new_moments = [d[0] for d in done], [d[1] for d in done]
     rules = [weight_rule(MATRIX_RATE * 0.2 * math.sqrt(w.shape[1])) for w in mats]
-    new_mats = [d[0] for d in finish(ortho_pieces, mats, rules, 1, nr)]
+    new_mats = [d[0] for d in finish(ortho_pieces, mats, rules, 1, nr, (0, 1, 2, 3))]
 
     inputs = tok.astype(F32)
-    block_out = (inputs + jnp.sum(summed.astype(F32), axis=0) + down_bias_full).astype(BF)
-    d_normed = jnp.sum(summed_normed.astype(F32), axis=0)
+    rest = local_len - cut
+    summed = jnp.concatenate([jnp.sum(x.astype(F32), axis=0) for x in (summed, late[:, local_len : local_len + rest])])
+    block_out = (inputs + summed + down_bias_full).astype(BF)
+    d_normed = jnp.sum(late[:, :local_len].astype(F32), axis=0)
     xhat, inv_std = layer_norm_parts(inputs)
     e = d_normed * gain
     input_grad = cot.astype(F32) + inv_std * (
         e - jnp.mean(e, axis=-1, keepdims=True) - xhat * jnp.mean(e * xhat, axis=-1, keepdims=True)
     )
 
-    pair = jnp.stack([jnp.sum(d_normed * xhat, axis=0), jnp.sum(d_normed, axis=0)])
-    pair = pair.reshape(2, nf, rows).transpose(1, 0, 2)
-    pair = jnp.sum(z_exchange(after(pair, back)), axis=0).reshape(2 * rows)
+    pair = jnp.sum(late[:, local_len + rest : local_len + rest + 2, :rows].astype(F32), axis=0).reshape(2 * rows)
     down_sum = jnp.sum(lax.dynamic_slice_in_dim(cot_all, f * rows, rows, 1).astype(F32), axis=0)
-    up_sum = jnp.sum(d_pre.astype(F32), axis=0)
+    up_sum = up_sum.reshape(hidden_width)
     small = plane_sum_small(jnp.concatenate([pair, down_sum, up_sum]), nr)
     vec_grads = [small[:rows], small[rows : 2 * rows], small[3 * rows :], small[2 * rows : 3 * rows]]
     vec_moments = [

time: 590 us -> 525 us (0.89)
  matrix products: 36.4 us -> 15.1 us
  local copies, waits for them, and re-layouts: 51.4 us -> 32.7 us
  other arithmetic: 45.6 us -> 27.2 us
  Pallas kernels: 156 us -> 174 us
  starting transfers between devices: 112 us -> 97.4 us
  waiting for transfers between devices: 180 us -> 167 us
    ppermute x52, waiting for transfers between devices: 104 us -> 58.6 us  [xor_swap(): return lax.ppermute(x, 'rep', [(i, i ^ mask) for i in range(nr)])]
    all_to_all x9 -> x8, waiting for transfers between devices: 43.5 us -> 62.7 us  [z_exchange(): return lax.all_to_all(x, 'fsdp', split_axis=0, concat_axis=0, tiled=True)]
    pallas_call x5 -> x8, Pallas kernels: 42.8 us -> 61 us  [the longest x1 21.6 us: attend_back(): pl.pallas_call(kernel, grid_spec=pltpu.PrefetchScalarGridSpec(num_scalar_...]
    ppermute x4, waiting for transfers between devices: 32.5 us -> 45.4 us  [z_gather(): lax.ppermute(left, 'fsdp', [(i, i - step) for i in range(step, nf - 1)])]
    dot_general x2 -> x0, matrix products: 12.2 us -> none  [the longest x1 6.22 us: on_device(): jnp.dot(normed, up_cols, preferred_element_type=F32) + up_bias.astype(F32)]
    all_to_all x9 -> x8, starting transfers between devices: 49.3 us -> 38.3 us  [z_exchange(): return lax.all_to_all(x, 'fsdp', split_axis=0, concat_axis=0, tiled=True)]
    add x6 -> x0, other arithmetic: 9.37 us -> none  [the longest x2 5.12 us: joined(): return mine + xor_swap(other, 1, nr).astype(F32)]
    dynamic_slice x6 -> x0, local copies, waits for them, and re-layouts: 7.09 us -> none  [the longest x4 6.19 us: halve(): mine = lax.dynamic_index_in_dim(x, rep_bit(bit), axis, keepdims=False)]
  transfers between devices with their start and end apart: 73 -> 72, of which waited for: 24 -> 25; matrix products, arithmetic and copies ran while one was open for 22% -> 11% of each run, Pallas kernels for 23% -> 25%
where the time goes in v1:
time: 525 us; the launch traced here: 515 us
  Pallas kernels  174 us (33%)
  waiting for transfers between devices  167 us (32%)
  starting transfers between devices  97.4 us (19%)
  local copies, waits for them, and re-layouts  32.7 us (6%)
  other arithmetic  27.2 us (5%)
  matrix products  15.1 us (3%)
    all_to_all x8, waiting for transfers between devices, z_exchange(): return lax.all_to_all(x, 'fsdp', split_axis=0, concat_axis=0, tiled=True)  62.7 us
    ppermute x52, waiting for transfers between devices, xor_swap(): return lax.ppermute(x, 'rep', [(i, i ^ mask) for i in range(nr)])  58.6 us
    pallas_call x1, Pallas kernels, orthogonalize(): pl.pallas_call(ortho_kernel, in_specs=[pl.BlockSpec(memory_space=pltpu.SM...  49 us
    ppermute x4, waiting for transfers between devices, z_gather(): lax.ppermute(left, 'fsdp', [(i, i - step) for i in range(step, nf - 1)])  45.4 us
    all_to_all x8, starting transfers between devices, z_exchange(): return lax.all_to_all(x, 'fsdp', split_axis=0, concat_axis=0, tiled=True)  38.3 us
    ppermute x52, starting transfers between devices, xor_swap(): return lax.ppermute(x, 'rep', [(i, i ^ mask) for i in range(nr)])  37.4 us
    pallas_call x2, Pallas kernels, finish(): pl.pallas_call(kernel, grid=(steps,), in_specs=[pl.BlockSpec(memory_space...  33.4 us
    pallas_call x1, Pallas kernels, attend_back(): pl.pallas_call(kernel, grid_spec=pltpu.PrefetchScalarGridSpec(num_scalar_...  21.6 us
  transfers between devices with their start and end apart: 72, of which 25 were waited for; matrix products, arithmetic and copies ran while one was open for 11% of the time, Pallas kernels for 25%

profile of v1, /device:TPU:0, one launch (start us, length us, event | category | flops | bytes accessed | tf_op | source)
XLA Modules:
  0.0 515.0 jit_solution(1431176500210904225)
XLA Ops:
  2.0 5.6 %collective-permute-start = (bf16[256,1024]{1,0:T(8,128)(2,1)}, bf16[256,1024]{1,0:T(8,128)(2,1)S(1)}, u32[]{:S(2)}, u32[]{:S(2)}) collective-permute-start(bf16[256,1024]{1,0:T(8,128)(2,1)} %bitcast.108), channel_id=1, source_target_pairs={{0,1},{1,2},{2,3},{4,5},{5,6},{6,7},{8,9},{9,10},{10,11},{12,13},{... | collective-permute-start | bytes 1572872 | tf_op jit(solution)/shard_map/ppermute | solution.py:38
  10.1 4.3 all-to-all-start
  15.6 8.6 %all-to-all-done = bf16[4,40,768]{2,1,0:T(8,128)(2,1)S(1)} async-done(((bf16[4,40,768]{2,1,0:T(8,128)(2,1)}), bf16[4,40,768]{2,1,0:T(8,128)(2,1)S(1)}, u32[]{:S(2)}, u32[]{:S(2)}) %all-to-all-start) | async-done | bytes 245792 | tf_op jit(solution)/shard_map/all_to_all | solution.py:56
  39.7 7.7 %all-to-all-start.1 = ((bf16[4,32,2048]{2,1,0:T(8,128)(2,1)}), bf16[4,32,2048]{2,1,0:T(8,128)(2,1)S(1)}, u32[]{:S(2)}, u32[]{:S(2)}) async-start(bf16[4,32,2048]{2,1,0:T(8,128)(2,1)} %pad_maximum_fusion.2), calls=%async_computation.1 | async-start | bytes 1048576 | tf_op jit(solution)/shard_map/all_to_all | solution.py:56
  48.7 5.4 %collective-permute-start.15 = (bf16[256,1024]{1,0:T(8,128)(2,1)}, bf16[256,1024]{1,0:T(8,128)(2,1)}, u32[]{:S(2)}, u32[]{:S(2)}) collective-permute-start(bf16[256,1024]{1,0:T(8,128)(2,1)} %bitcast.8), channel_id=1, source_target_pairs={{0,1},{1,2},{2,3},{4,5},{5,6},{6,7},{8,9},{9,10},{10,11},{12,13},{... | collective-permute-start | bytes 1572872 | tf_op jit(solution)/shard_map/ppermute | solution.py:38
  59.7 32.8 %collective-permute-done.4 = bf16[256,1024]{1,0:T(8,128)(2,1)S(1)} collective-permute-done((bf16[256,1024]{1,0:T(8,128)(2,1)S(1)}, bf16[256,1024]{1,0:T(8,128)(2,1)S(1)}, u32[]{:S(2)}, u32[]{:S(2)}) %collective-permute-start.4) | collective-permute-done | bytes 524320 | tf_op jit(solution)/shard_map/ppermute | solution.py:50
  108.5 14.0 %attend.1 = (bf16[1024,256]{1,0:T(8,128)(2,1)}, bf16[1024,256]{1,0:T(8,128)(2,1)}, bf16[1024,256]{1,0:T(8,128)(2,1)}, bf16[4,1024,1024]{2,1,0:T(8,128)(2,1)}, bf16[1024,256]{1,0:T(8,128)(2,1)}) custom-call(f32[1024,768]{1,0:T(8,128)} %fusion.52.qf_ref.kf_ref.vf_ref, f32[1024,768]{1,0:T(8,128)} %fusion.52.qf_ref.kf_ref.vf_ref, ...), custom_call_target="tpu_custom_call" | custom-call | tf_op jit(solution)/shard_map/attend/pallas_call | solution.py:165
  128.6 12.6 %collective-permute-done.19 = bf16[256,1024]{1,0:T(8,128)(2,1)S(1)} collective-permute-done((bf16[256,1024]{1,0:T(8,128)(2,1)}, bf16[256,1024]{1,0:T(8,128)(2,1)S(1)}, u32[]{:S(2)}, u32[]{:S(2)}) %collective-permute-start.19) | collective-permute-done | bytes 524320 | tf_op jit(solution)/shard_map/ppermute | solution.py:50
  149.0 4.2 shard_map.378
  153.3 17.6 %feed_forward.1 = (bf16[1024,1024]{1,0:T(8,128)(2,1)}, bf16[1024,1024]{1,0:T(8,128)(2,1)}, f32[1,1024]{1,0:T(1,128)}, bf16[2,4,128,1024]{3,2,1,0:T(8,128)(2,1)},...) custom-call(s32[1]{0:T(128)} %bitcast.7.w_ref, bf16[1024,1024]{1,0:T(8,128)(2,1)} %copy-done.15, ...), custom_call_target="tpu_custom_call" | custom-call | flops 8589934592 | bytes 20971520 | tf_op jit(solution)/shard_map/feed_forward/pallas_call | solution.py:515
  174.3 3.8 moment_units.1
  178.1 4.2 all-to-all-start.2
  183.7 5.4 %shard_map.379 = (bf16[2,128,1024]{2,1,0:T(8,128)(2,1)}, f32[2,128,1024]{2,1,0:T(8,128)}, bf16[2,128,1024]{2,1,0:T(8,128)(2,1)}, f32[2,128,1024]{2,1,0:T(8,128)}) custom-call(s32[1]{0:T(128)} %bitcast.5.r_ref, f32[4,128,1024]{2,1,0:T(8,128)} %get-tuple-element.105.refs_0_, bf16[2,4,128,1024]{3,2,1,0:T(8,128)(2,1)} %copy-done.3, ...), custom_call_target="tpu_custom_call" | custom-call | tf_op jit(solution)/shard_map/pallas_call | solution.py:579
  191.2 21.6 %attend_back.1 = (bf16[3,256,1024]{2,1,0:T(8,128)(2,1)}, bf16[2,2,1,128,1024]{4,3,2,1,0:T(8,128)(2,1)}, f32[2,2,1,128,1024]{4,3,2,1,0:T(8,128)}) custom-call(s32[1]{0:T(128)} %bitcast.7.w_ref, bf16[1024,256]{1,0:T(8,128)(2,1)} %get-tuple-element.112.q_ref, bf16[1024,256]{1,0:T(8,128)(2,1)} %get-tuple-element.113.k_ref, ...), custom_call_target="tpu_custom_call" | custom-call | flops 6442450944 | bytes 8388608 | tf_op jit(solution)/shard_map/attend_back/pallas_call | solution.py:231
  220.6 5.0 all-to-all-start.3
  234.1 4.1 shard_map.381
  242.3 5.3 %collective-permute-done.34.refs_1_ = bf16[2,64,1024]{2,1,0:T(8,128)(2,1)S(1)} collective-permute-done((bf16[2,64,1024]{2,1,0:T(8,128)(2,1)}, bf16[2,64,1024]{2,1,0:T(8,128)(2,1)S(1)}, u32[]{:S(2)}, u32[]{:S(2)}) %collective-permute-start.34) | collective-permute-done | bytes 262176 | tf_op jit(solution)/shard_map/ppermute | solution.py:60
  261.6 5.1 all-to-all-start.4
  266.7 22.5 %all-to-all-done.4.g_ref = bf16[4,1024,128]{2,1,0:T(8,128)(2,1)S(1)} async-done(((bf16[4,1024,128]{2,1,0:T(8,128)(2,1)}), bf16[4,1024,128]{2,1,0:T(8,128)(2,1)S(1)}, u32[]{:S(2)}, u32[]{:S(2)}) %all-to-all-start.4) | async-done | bytes 1048608 | tf_op jit(solution)/shard_map/all_to_all | solution.py:56
  295.4 4.7 fusion.10
  301.5 15.1 %collective-permute-done.41.refs_2_ = bf16[1024,512]{1,0:T(8,128)(2,1)S(1)} collective-permute-done((bf16[1024,512]{1,0:T(8,128)(2,1)}, bf16[1024,512]{1,0:T(8,128)(2,1)S(1)}, u32[]{:S(2)}, u32[]{:S(2)}) %collective-permute-start.41) | collective-permute-done | bytes 1048608 | tf_op jit(solution)/shard_map/ppermute | solution.py:60
  320.3 3.8 fusion.7
  329.9 6.6 %gram.1.ga_ref = f32[10,256,256]{2,1,0:T(8,128)} custom-call(bf16[1024,512]{1,0:T(8,128)(2,1)} %momentum_cols.1.refs_0_.s_ref, bf16[1024,512]{1,0:T(8,128)(2,1)} %copy-done.42, bf16[1024,512]{1,0:T(8,128)(2,1)} %copy-done.41, bf16[512,512]{1,0:T(8,128)(2,1)} %copy-done.60, bf16[512,512]{1,0:T(8,128)(2,1)} %collective-permute-done.43.refs_4_), custom_call_target="tpu_custom_call" | custom-call | flops 4294967296 | bytes 4194304 | tf_op jit(solution)/shard_map/gram/pallas_call | solution.py:303
  340.1 21.0 %all-to-all-done.5 = bf16[4,3,256,128]{3,2,1,0:T(8,128)(2,1)S(1)} async-done(((bf16[4,3,256,128]{3,2,1,0:T(8,128)(2,1)}), bf16[4,3,256,128]{3,2,1,0:T(8,128)(2,1)S(1)}, u32[]{:S(2)}, u32[]{:S(2)}) %all-to-all-start.5) | async-done | bytes 786464 | tf_op jit(solution)/shard_map/all_to_all | solution.py:56
  362.0 4.1 all-to-all-start.6
  372.9 49.0 %orthogonalize.1 = bf16[4,256,512]{2,1,0:T(8,128)(2,1)} custom-call(s32[1]{0:T(128)} %bitcast.31.flag_ref, f32[10,256,256]{2,1,0:T(8,128)} %gram.1.ga_ref, f32[10,256,256]{2,1,0:T(8,128)} %collective-permute-done.44.gb_ref, bf16[1024,512]{1,0:T(8,128)(2,1)} %momentum_cols.1.refs_0_.s_ref), custom_call_target="tpu_custom_call" | custom-call | flops 42949672960 | bytes 8388608 | tf_op jit(solution)/shard_map/orthogonalize/pallas_call | solution.py:395
  422.0 10.6 %all-to-all-done.6 = bf16[4,360,1024]{2,1,0:T(8,128)(2,1)S(1)} async-done(((bf16[4,360,1024]{2,1,0:T(8,128)(2,1)}), bf16[4,360,1024]{2,1,0:T(8,128)(2,1)S(1)}, u32[]{:S(2)}, u32[]{:S(2)}) %all-to-all-start.6) | async-done | bytes 2949152 | tf_op jit(solution)/shard_map/all_to_all | solution.py:56
  432.6 4.3 all-to-all-start.7
  443.1 19.3 %shard_map.383 = (f32[256,3072]{1,0:T(8,128)}, f32[256,3072]{1,0:T(8,128)}, f32[256,1024]{1,0:T(8,128)}, f32[256,1024]{1,0:T(8,128)}, f32[256,4096]{1,0:T(8,128)...) custom-call(s32[1]{0:T(128)} %bitcast.5.r_ref, bf16[3,256,512]{2,1,0:T(8,128)(2,1)} %pad_maximum_fusion.refs_0_, ...), custom_call_target="tpu_custom_call" | custom-call | flops 6553600 | bytes 44040192 | tf_op jit(solution)/shard_map/pallas_call | solution.py:756
  470.8 15.1 %collective-permute-done.53 = f32[1792]{0:T(1024)S(1)} collective-permute-done((f32[1792]{0:T(1024)S(1)}, f32[1792]{0:T(1024)S(1)}, u32[]{:S(2)}, u32[]{:S(2)}) %collective-permute-start.53) | collective-permute-done | bytes 7200 | tf_op jit(solution)/shard_map/ppermute | solution.py:60
  492.6 4.0 collective-permute-done.60.refs_6_
  500.7 14.1 %shard_map.384 = (f32[256,3072]{1,0:T(8,128)}, f32[256,1024]{1,0:T(8,128)}, f32[256,4096]{1,0:T(8,128)}, f32[256,4096]{1,0:T(8,128)}) custom-call(s32[1]{0:T(128)} %bitcast.5.r_ref, bf16[3,256,512]{2,1,0:T(8,128)(2,1)} %copy-done.8, bf16[3,256,512]{2,1,0:T(8,128)(2,1)} %copy-done.23, bf16[3,256,512]{2,1,0:T(8,128)(2,1)} %copy-done.17, ...), custom_call_target="tpu_custom_call" | custom-call | flops 6553600 | bytes 31457280 | tf_op jit(solution)/shard_map/pallas_call | solution.py:756
  (355 shorter events, 151.3 us)
Async XLA Ops:
  0.7 33.5 %collective-permute-start.3 = (bf16[256,1024]{1,0:T(8,128)(2,1)}, bf16[256,1024]{1,0:T(8,128)(2,1)S(1)}, u32[]{:S(2)}, u32[]{:S(2)}) collective-permute-start(bf16[256,1024]{1,0:T(8,128)(2,1)} %bitcast.107), channel_id=1, source_target_pairs={{1,0},{2,1},{3,2},{5,4},{6,5},{7,6},{9,8},{10,9},{11,10},{13,12},{... | collective-permute-start | bytes 1572872 | tf_op jit(solution)/shard_map/ppermute | solution.py:39
  2.0 26.2 %collective-permute-start = (bf16[256,1024]{1,0:T(8,128)(2,1)}, bf16[256,1024]{1,0:T(8,128)(2,1)S(1)}, u32[]{:S(2)}, u32[]{:S(2)}) collective-permute-start(bf16[256,1024]{1,0:T(8,128)(2,1)} %bitcast.108), channel_id=1, source_target_pairs={{0,1},{1,2},{2,3},{4,5},{5,6},{6,7},{8,9},{9,10},{10,11},{12,13},{... | collective-permute-start | bytes 1572872 | tf_op jit(solution)/shard_map/ppermute | solution.py:38
  28.2 30.0 %collective-permute-start.1 = (bf16[256,1024]{1,0:T(8,128)(2,1)S(1)}, bf16[256,1024]{1,0:T(8,128)(2,1)S(1)}, u32[]{:S(2)}, u32[]{:S(2)}) collective-permute-start(bf16[256,1024]{1,0:T(8,128)(2,1)S(1)} %collective-permute-done), channel_id=1, source_target_pairs={{1,3},{5,7},{9,11},{13,15},{17,19},{21,23},{25,27},{29,31}} | collective-permute-start | bytes 1572872 | tf_op jit(solution)/shard_map/ppermute | solution.py:49
  32.5 27.0 %collective-permute-start.2 = (bf16[256,1024]{1,0:T(8,128)(2,1)S(1)}, bf16[256,1024]{1,0:T(8,128)(2,1)S(1)}, u32[]{:S(2)}, u32[]{:S(2)}) collective-permute-start(bf16[256,1024]{1,0:T(8,128)(2,1)S(1)} %collective-permute-done), channel_id=1, source_target_pairs={{1,2},{2,3},{5,6},{6,7},{9,10},{10,11},{13,14},{14,15},{17,18},{18... | collective-permute-start | bytes 1572872 | tf_op jit(solution)/shard_map/ppermute | solution.py:49
  39.7 62.3 %all-to-all-start.1 = ((bf16[4,32,2048]{2,1,0:T(8,128)(2,1)}), bf16[4,32,2048]{2,1,0:T(8,128)(2,1)S(1)}, u32[]{:S(2)}, u32[]{:S(2)}) async-start(bf16[4,32,2048]{2,1,0:T(8,128)(2,1)} %pad_maximum_fusion.2), calls=%async_computation.1 | async-start | bytes 1048576 | tf_op jit(solution)/shard_map/all_to_all | solution.py:56
  47.4 52.5 %collective-permute-start.16 = (bf16[256,1024]{1,0:T(8,128)(2,1)}, bf16[256,1024]{1,0:T(8,128)(2,1)}, u32[]{:S(2)}, u32[]{:S(2)}) collective-permute-start(bf16[256,1024]{1,0:T(8,128)(2,1)} %bitcast.8), channel_id=1, source_target_pairs={{1,0},{2,1},{3,2},{5,4},{6,5},{7,6},{9,8},{10,9},{11,10},{13,12},{... | collective-permute-start | bytes 1572872 | tf_op jit(solution)/shard_map/ppermute | solution.py:39
  48.7 51.2 %collective-permute-start.15 = (bf16[256,1024]{1,0:T(8,128)(2,1)}, bf16[256,1024]{1,0:T(8,128)(2,1)}, u32[]{:S(2)}, u32[]{:S(2)}) collective-permute-start(bf16[256,1024]{1,0:T(8,128)(2,1)} %bitcast.8), channel_id=1, source_target_pairs={{0,1},{1,2},{2,3},{4,5},{5,6},{6,7},{8,9},{9,10},{10,11},{12,13},{... | collective-permute-start | bytes 1572872 | tf_op jit(solution)/shard_map/ppermute | solution.py:38
  54.1 38.5 %collective-permute-start.5 = (bf16[256,1024]{1,0:T(8,128)(2,1)S(1)}, bf16[256,1024]{1,0:T(8,128)(2,1)}, u32[]{:S(2)}, u32[]{:S(2)}) collective-permute-start(bf16[256,1024]{1,0:T(8,128)(2,1)S(1)} %collective-permute-done.3), channel_id=1, source_target_pairs={{2,0},{6,4},{10,8},{14,12},{18,16},{22,20},{26,24},{30,28}} | collective-permute-start | bytes 1572872 | tf_op jit(solution)/shard_map/ppermute | solution.py:50
  58.2 34.4 %collective-permute-start.4 = (bf16[256,1024]{1,0:T(8,128)(2,1)S(1)}, bf16[256,1024]{1,0:T(8,128)(2,1)S(1)}, u32[]{:S(2)}, u32[]{:S(2)}) collective-permute-start(bf16[256,1024]{1,0:T(8,128)(2,1)S(1)} %collective-permute-done.3), channel_id=1, source_target_pairs={{1,0},{2,1},{5,4},{6,5},{9,8},{10,9},{13,12},{14,13},{17,16},{18,1... | collective-permute-start | bytes 1572872 | tf_op jit(solution)/shard_map/ppermute | solution.py:50
  99.9 22.5 %collective-permute-start.17 = (bf16[256,1024]{1,0:T(8,128)(2,1)}, bf16[256,1024]{1,0:T(8,128)(2,1)S(1)}, u32[]{:S(2)}, u32[]{:S(2)}) collective-permute-start(bf16[256,1024]{1,0:T(8,128)(2,1)} %collective-permute-done.15), channel_id=1, source_target_pairs={{1,3},{5,7},{9,11},{13,15},{17,19},{21,23},{25,27},{29,31}} | collective-permute-start | bytes 1572872 | tf_op jit(solution)/shard_map/ppermute | solution.py:49
  100.6 23.3 %collective-permute-start.18 = (bf16[256,1024]{1,0:T(8,128)(2,1)}, bf16[256,1024]{1,0:T(8,128)(2,1)S(1)}, u32[]{:S(2)}, u32[]{:S(2)}) collective-permute-start(bf16[256,1024]{1,0:T(8,128)(2,1)} %collective-permute-done.15), channel_id=1, source_target_pairs={{1,2},{2,3},{5,6},{6,7},{9,10},{10,11},{13,14},{14,15},{17,18},{18... | collective-permute-start | bytes 1572872 | tf_op jit(solution)/shard_map/ppermute | solution.py:49
  102.0 23.2 %collective-permute-start.24 = (bf16[4,32,2048]{2,1,0:T(8,128)(2,1)S(1)}, bf16[4,32,2048]{2,1,0:T(8,128)(2,1)S(1)}, u32[]{:S(2)}, u32[]{:S(2)}) collective-permute-start(bf16[4,32,2048]{2,1,0:T(8,128)(2,1)S(1)} %all-to-all-done.1.refs_0_), channel_id=1, source_target_pairs={{0,16},{4,20},{8,24},{12,28},{16,0},{20,4},{24,8},{28,12},{1,17},{... | collective-permute-start | bytes 1572872 | tf_op jit(solution)/shard_map/ppermute | solution.py:60
  103.3 23.3 %collective-permute-start.22 = (bf16[4,32,2048]{2,1,0:T(8,128)(2,1)S(1)}, bf16[4,32,2048]{2,1,0:T(8,128)(2,1)S(1)}, u32[]{:S(2)}, u32[]{:S(2)}) collective-permute-start(bf16[4,32,2048]{2,1,0:T(8,128)(2,1)S(1)} %all-to-all-done.1.refs_0_), channel_id=1, source_target_pairs={{0,8},{4,12},{8,0},{12,4},{16,24},{20,28},{24,16},{28,20},{1,9},{5... | collective-permute-start | bytes 1572872 | tf_op jit(solution)/shard_map/ppermute | solution.py:60
  107.2 21.3 %collective-permute-start.20 = (bf16[256,1024]{1,0:T(8,128)(2,1)}, bf16[256,1024]{1,0:T(8,128)(2,1)}, u32[]{:S(2)}, u32[]{:S(2)}) collective-permute-start(bf16[256,1024]{1,0:T(8,128)(2,1)} %collective-permute-done.16), channel_id=1, source_target_pairs={{2,0},{6,4},{10,8},{14,12},{18,16},{22,20},{26,24},{30,28}} | collective-permute-start | bytes 1572872 | tf_op jit(solution)/shard_map/ppermute | solution.py:50
  124.0 23.4 %collective-permute-start.21 = (bf16[4,32,2048]{2,1,0:T(8,128)(2,1)S(1)}, bf16[4,32,2048]{2,1,0:T(8,128)(2,1)S(1)}, u32[]{:S(2)}, u32[]{:S(2)}) collective-permute-start(bf16[4,32,2048]{2,1,0:T(8,128)(2,1)S(1)} %all-to-all-done.1.refs_0_), channel_id=1, source_target_pairs={{0,4},{4,0},{8,12},{12,8},{16,20},{20,16},{24,28},{28,24},{1,5},{5... | collective-permute-start | bytes 1572872 | tf_op jit(solution)/shard_map/ppermute | solution.py:60
  178.1 42.4 %all-to-all-start.2 = ((bf16[4,256,512]{2,1,0:T(8,128)(2,1)}), bf16[4,256,512]{2,1,0:T(8,128)(2,1)}, u32[]{:S(2)}, u32[]{:S(2)}) async-start(bf16[4,256,512]{2,1,0:T(8,128)(2,1)} %moment_units.1), calls=%async_computation.2 | async-start | bytes 2097152 | tf_op jit(solution)/shard_map/all_to_all | solution.py:56
  189.1 36.5 %collective-permute-start.31 = (bf16[2,128,1024]{2,1,0:T(8,128)(2,1)}, bf16[2,128,1024]{2,1,0:T(8,128)(2,1)S(1)}, u32[]{:S(2)}, u32[]{:S(2)}) collective-permute-start(bf16[2,128,1024]{2,1,0:T(8,128)(2,1)} %get-tuple-element.108), channel_id=1, source_target_pairs={{0,8},{4,12},{8,0},{12,4},{16,24},{20,28},{24,16},{28,20},{1,9},{5... | collective-permute-start | bytes 1572872 | tf_op jit(solution)/shard_map/ppermute | solution.py:60
  190.4 35.2 %collective-permute-start.32 = (bf16[2,128,1024]{2,1,0:T(8,128)(2,1)}, bf16[2,128,1024]{2,1,0:T(8,128)(2,1)S(1)}, u32[]{:S(2)}, u32[]{:S(2)}) collective-permute-start(bf16[2,128,1024]{2,1,0:T(8,128)(2,1)} %get-tuple-element.110), channel_id=1, source_target_pairs={{0,16},{4,20},{8,24},{12,28},{16,0},{20,4},{24,8},{28,12},{1,17},{... | collective-permute-start | bytes 1572872 | tf_op jit(solution)/shard_map/ppermute | solution.py:60
  220.6 41.0 %all-to-all-start.3 = ((bf16[4,160,1024]{2,1,0:T(8,128)(2,1)}), bf16[4,160,1024]{2,1,0:T(8,128)(2,1)S(1)}, u32[]{:S(2)}, u32[]{:S(2)}) async-start(bf16[4,160,1024]{2,1,0:T(8,128)(2,1)} %slice.277), calls=%async_computation.3 | async-start | bytes 2621440 | tf_op jit(solution)/shard_map/all_to_all | solution.py:56
  261.6 27.6 %all-to-all-start.4 = ((bf16[4,1024,128]{2,1,0:T(8,128)(2,1)}), bf16[4,1024,128]{2,1,0:T(8,128)(2,1)S(1)}, u32[]{:S(2)}, u32[]{:S(2)}) async-start(bf16[4,1024,128]{2,1,0:T(8,128)(2,1)} %get-tuple-element.141), calls=%async_computation.4 | async-start | bytes 2097152 | tf_op jit(solution)/shard_map/all_to_all | solution.py:56
  293.2 23.5 %collective-permute-start.41 = (bf16[1024,512]{1,0:T(8,128)(2,1)}, bf16[1024,512]{1,0:T(8,128)(2,1)S(1)}, u32[]{:S(2)}, u32[]{:S(2)}) collective-permute-start(bf16[1024,512]{1,0:T(8,128)(2,1)} %momentum_cols.1.refs_0_.s_ref), channel_id=1, source_target_pairs={{0,16},{4,20},{8,24},{12,28},{16,0},{20,4},{24,8},{28,12},{1,17},{... | collective-permute-start | bytes 3145736 | tf_op jit(solution)/shard_map/ppermute | solution.py:60
  294.2 23.7 %collective-permute-start.40 = (bf16[1024,512]{1,0:T(8,128)(2,1)}, bf16[1024,512]{1,0:T(8,128)(2,1)S(1)}, u32[]{:S(2)}, u32[]{:S(2)}) collective-permute-start(bf16[1024,512]{1,0:T(8,128)(2,1)} %momentum_cols.1.refs_0_.s_ref), channel_id=1, source_target_pairs={{0,8},{4,12},{8,0},{12,4},{16,24},{20,28},{24,16},{28,20},{1,9},{5... | collective-permute-start | bytes 3145736 | tf_op jit(solution)/shard_map/ppermute | solution.py:60
  336.5 36.4 %collective-permute-start.44 = (f32[10,256,256]{2,1,0:T(8,128)}, f32[10,256,256]{2,1,0:T(8,128)}, u32[]{:S(2)}, u32[]{:S(2)}) collective-permute-start(f32[10,256,256]{2,1,0:T(8,128)} %gram.1.ga_ref), channel_id=1, source_target_pairs={{0,4},{4,0},{8,12},{12,8},{16,20},{20,16},{24,28},{28,24},{1,5},{5... | collective-permute-start | bytes 7864328 | tf_op jit(solution)/shard_map/ppermute | solution.py:60
  336.6 24.5 %all-to-all-start.5 = ((bf16[4,3,256,128]{3,2,1,0:T(8,128)(2,1)}), bf16[4,3,256,128]{3,2,1,0:T(8,128)(2,1)S(1)}, u32[]{:S(2)}, u32[]{:S(2)}) async-start(bf16[4,3,256,128]{3,2,1,0:T(8,128)(2,1)} %get-tuple-element.145), calls=%async_computation.5 | async-start | bytes 1572864 | tf_op jit(solution)/shard_map/all_to_all | solution.py:56
  362.0 70.6 %all-to-all-start.6 = ((bf16[4,360,1024]{2,1,0:T(8,128)(2,1)}), bf16[4,360,1024]{2,1,0:T(8,128)(2,1)S(1)}, u32[]{:S(2)}, u32[]{:S(2)}) async-start(bf16[4,360,1024]{2,1,0:T(8,128)(2,1)} %fusion.9), calls=%async_computation.6 | async-start | bytes 5898240 | tf_op jit(solution)/shard_map/all_to_all | solution.py:56
  369.4 67.7 %collective-permute-start.50 = (bf16[3,256,512]{2,1,0:T(8,128)(2,1)}, bf16[3,256,512]{2,1,0:T(8,128)(2,1)}, u32[]{:S(2)}, u32[]{:S(2)}) collective-permute-start(bf16[3,256,512]{2,1,0:T(8,128)(2,1)} %pad_maximum_fusion.refs_0_), channel_id=1, source_target_pairs={{0,24},{4,28},{8,16},{12,20},{16,8},{20,12},{24,0},{28,4},{1,25},{... | collective-permute-start | bytes 2359304 | tf_op jit(solution)/shard_map/ppermute | solution.py:60
  371.2 66.4 %collective-permute-start.48 = (bf16[3,256,512]{2,1,0:T(8,128)(2,1)}, bf16[3,256,512]{2,1,0:T(8,128)(2,1)}, u32[]{:S(2)}, u32[]{:S(2)}) collective-permute-start(bf16[3,256,512]{2,1,0:T(8,128)(2,1)} %pad_maximum_fusion.refs_0_), channel_id=1, source_target_pairs={{0,16},{4,20},{8,24},{12,28},{16,0},{20,4},{24,8},{28,12},{1,17},{... | collective-permute-start | bytes 2359304 | tf_op jit(solution)/shard_map/ppermute | solution.py:60
  371.8 65.9 %collective-permute-start.46 = (bf16[3,256,512]{2,1,0:T(8,128)(2,1)}, bf16[3,256,512]{2,1,0:T(8,128)(2,1)}, u32[]{:S(2)}, u32[]{:S(2)}) collective-permute-start(bf16[3,256,512]{2,1,0:T(8,128)(2,1)} %pad_maximum_fusion.refs_0_), channel_id=1, source_target_pairs={{0,8},{4,12},{8,0},{12,4},{16,24},{20,28},{24,16},{28,20},{1,9},{5... | collective-permute-start | bytes 2359304 | tf_op jit(solution)/shard_map/ppermute | solution.py:60
  432.6 29.9 %all-to-all-start.7 = ((bf16[4,256,512]{2,1,0:T(8,128)(2,1)}), bf16[4,256,512]{2,1,0:T(8,128)(2,1)}, u32[]{:S(2)}, u32[]{:S(2)}) async-start(bf16[4,256,512]{2,1,0:T(8,128)(2,1)} %orthogonalize.1), calls=%async_computation.7 | async-start | bytes 2097152 | tf_op jit(solution)/shard_map/all_to_all | solution.py:56
  465.2 21.6 %collective-permute-start.58 = (bf16[3,256,512]{2,1,0:T(8,128)(2,1)S(1)}, bf16[3,256,512]{2,1,0:T(8,128)(2,1)S(1)}, u32[]{:S(2)}, u32[]{:S(2)}) collective-permute-start(bf16[3,256,512]{2,1,0:T(8,128)(2,1)S(1)} %pad_maximum_fusion.1.refs_0_), channel_id=1, source_target_pairs={{0,16},{4,20},{8,24},{12,28},{16,0},{20,4},{24,8},{28,12},{1,17},{... | collective-permute-start | bytes 2359304 | tf_op jit(solution)/shard_map/ppermute | solution.py:60
  466.4 21.4 %collective-permute-start.56 = (bf16[3,256,512]{2,1,0:T(8,128)(2,1)S(1)}, bf16[3,256,512]{2,1,0:T(8,128)(2,1)S(1)}, u32[]{:S(2)}, u32[]{:S(2)}) collective-permute-start(bf16[3,256,512]{2,1,0:T(8,128)(2,1)S(1)} %pad_maximum_fusion.1.refs_0_), channel_id=1, source_target_pairs={{0,8},{4,12},{8,0},{12,4},{16,24},{20,28},{24,16},{28,20},{1,9},{5... | collective-permute-start | bytes 2359304 | tf_op jit(solution)/shard_map/ppermute | solution.py:60
  467.5 31.2 %collective-permute-start.55 = (bf16[3,256,512]{2,1,0:T(8,128)(2,1)S(1)}, bf16[3,256,512]{2,1,0:T(8,128)(2,1)S(1)}, u32[]{:S(2)}, u32[]{:S(2)}) collective-permute-start(bf16[3,256,512]{2,1,0:T(8,128)(2,1)S(1)} %pad_maximum_fusion.1.refs_0_), channel_id=1, source_target_pairs={{0,4},{4,0},{8,12},{12,8},{16,20},{20,16},{24,28},{28,24},{1,5},{5... | collective-permute-start | bytes 2359304 | tf_op jit(solution)/shard_map/ppermute | solution.py:60
  (105 other events, 893.7 us)
